TPU v7x, 256 devices: a whole 4x4x8 slice. The times are simulated.
256 devices in a mesh: wide: 32 (over z, x_lo, core), narrow: 8 (over y, x_hi).
Axes of the slice: x: 4 (x_hi: 2, x_lo: 2; x = x_hi * 2 + x_lo), y: 4, z: 8, core: 2. Of those that a mesh axis runs over, the one named last changes fastest.
Arguments:
- design: float32 [384, 384, 384], P('wide', 'narrow'), may hold values from 0 to 1
- passive: int32 [384, 384, 384], P('wide', 'narrow'), may hold values 0 or 1
- displacement: float32 [3, 3, 128, 128, 128], P(None, None, 'wide', 'narrow'), may hold values from -6 to 6
- support: int32 [128, 128, 128], P('wide', 'narrow'), may hold values 0 or 1
- loading: int32 [128, 128, 128], P('wide', 'narrow'), may hold values 0 or 1
Outputs:
- residual: float32 [3, 3, 128, 128, 128], P(None, None, 'wide', 'narrow')
- compliance: float32 [3], replicated
- sensitivity: float32 [384, 384, 384], P('wide', 'narrow')
All inputs are finite; a program needn't handle non-finite values. No bound on the sum of `passive` or of `support` or of `loading` on one device may be relied on, other than what follows from the above.
Results may differ from a plain program's by a relative error of at most 0.0001.
Values sent between devices are 32-bit elements; how exact they have to be, the bound alone decides.
A program may use at most 64 MiB of HBM per device.

v0:
```python
import functools
import math

import jax
import jax.numpy as jnp
import numpy as np
from jax import lax
from jax.sharding import Mesh
from jax.sharding import PartitionSpec as P

RAD = 3
WIDE = ("wide_0", "wide_1", "wide_2")
NARROW = ("narrow_0", "narrow_1")
WIDE_NARROW = ("wide_0", "wide_1", "wide_2", "narrow_0", "narrow_1")


sharpness = 8.0
thresholds = (0.7, 0.5, 0.3)
stiff_floor = 0.001
load_force = 4.0
poisson = 0.3


def with_halo(shard, sides, width):
    for axis, dim in sides:
        count, length = (lax.axis_size(axis), shard.shape[dim])
        up = [(i, (i + 1) % count) for i in range(count - 1)]
        down = [(j, i) for i, j in up]
        last = lax.slice_in_dim(shard, length - width, length, axis=dim)
        initial = lax.slice_in_dim(shard, 0, width, axis=dim)
        before = lax.ppermute(last, axis, up)
        after = lax.ppermute(initial, axis, down)
        shard = jnp.concatenate([before, shard, after], axis=dim)
    return shard


def passed_along(block, axis, distance):
    devices = range(lax.axis_size(axis))
    route = [(i - distance, i) for i in devices if i - distance in devices]
    return lax.ppermute(block, axis, route)


def over_axes(shard, axes):
    return functools.reduce(lax.psum, axes, shard)


def element_matrix():
    inv_root = 1.0 / np.sqrt(3.0)
    elastic_scale = 1.0 / ((1.0 + poisson) * (1.0 - 2.0 * poisson))
    elastic = np.zeros((6, 6))
    for row_i in range(3):
        for col_j in range(3):
            elastic[row_i, col_j] = poisson
        elastic[row_i, row_i] = 1.0 - poisson
    for row_i in range(3, 6):
        elastic[row_i, row_i] = 0.5 - poisson
    elastic = elastic * elastic_scale
    corner_signs = [
        (2 * (corner // 4) - 1, 2 * (corner // 2 % 2) - 1, 2 * (corner % 2) - 1)
        for corner in range(8)
    ]
    stiffness = np.zeros((24, 24))
    for gauss_a in (-inv_root, inv_root):
        for gauss_b in (-inv_root, inv_root):
            for gauss_c in (-inv_root, inv_root):
                gauss_point = (gauss_a, gauss_b, gauss_c)
                derivs = np.zeros((8, 3))
                for corner in range(8):
                    for along in range(3):
                        slope_value = corner_signs[corner][along] / 8.0
                        for second in range(3):
                            if second != along:
                                slope_value = slope_value * (
                                    1.0 + corner_signs[corner][second] * gauss_point[second]
                                )
                        derivs[corner, along] = 2.0 * slope_value
                strain = np.zeros((6, 24))
                for corner in range(8):
                    column = 3 * corner
                    strain[0, column] = derivs[corner, 0]
                    strain[1, column + 1] = derivs[corner, 1]
                    strain[2, column + 2] = derivs[corner, 2]
                    strain[3, column] = derivs[corner, 1]
                    strain[3, column + 1] = derivs[corner, 0]
                    strain[4, column + 1] = derivs[corner, 2]
                    strain[4, column + 2] = derivs[corner, 1]
                    strain[5, column] = derivs[corner, 2]
                    strain[5, column + 2] = derivs[corner, 0]
                stiffness = stiffness + strain.T @ elastic @ strain * 0.125
    return stiffness.astype(np.float32)


def blur_axis(padded, axis_dim, length):
    summed = float(1 - RAD + RAD) * lax.slice_in_dim(padded, 0, length, axis=axis_dim)
    for offset in range(1, 2 * RAD + 1):
        summed = summed + float(RAD + 1 - abs(offset - RAD)) * lax.slice_in_dim(
            padded, offset, offset + length, axis=axis_dim
        )
    return summed


def edge_weights(start_index, amount, extent):
    places = start_index + jnp.arange(amount, dtype=jnp.int32)
    summed = jnp.zeros((amount,), jnp.float32)
    for offset in range(-RAD, RAD + 1):
        inside = ((places + offset >= 0) & (places + offset < extent)).astype(jnp.float32)
        summed = summed + float(RAD + 1 - abs(offset)) * inside
    return summed


def smooth_field(source):
    rows_out, cols_out, depth_out = source.shape
    padded = with_halo(source, ((WIDE, 0),), RAD)
    rowwise = blur_axis(padded, 0, rows_out)
    padded_cols = with_halo(rowwise, ((NARROW, 1),), RAD)
    colwise = blur_axis(padded_cols, 1, cols_out)
    deepened = jnp.pad(colwise, ((0, 0), (0, 0), (RAD, RAD)))
    return blur_axis(deepened, 2, depth_out)


def project(blurred, threshold):
    low_end = float(math.tanh(sharpness * threshold))
    denominator = low_end + float(math.tanh(sharpness * (1.0 - threshold)))
    steep_part = jnp.tanh(sharpness * (blurred - threshold))
    return (
        (low_end + steep_part) / denominator,
        sharpness * (1.0 - steep_part * steep_part) / denominator,
    )


def depth_averaging(fine_len, coarse_len):
    rows_index = jnp.arange(fine_len, dtype=jnp.int32)[:, None] // 3
    cols_index = jnp.arange(coarse_len, dtype=jnp.int32)[None, :]
    return (rows_index == cols_index).astype(jnp.float32)


def aggregate(fine_stiff, coarse_averaging, count_x, count_y):
    merged = jnp.dot(
        fine_stiff.reshape(-1, fine_stiff.shape[2]),
        coarse_averaging,
        precision=lax.Precision.HIGHEST,
    )
    merged = merged.reshape(count_x, 3, count_y, 3, coarse_averaging.shape[1])
    return jnp.sum(merged, axis=(1, 3)) / 27.0


def spread(coarse, coarse_averaging):
    count_x, count_y, count_z = coarse.shape
    deepened = jnp.dot(
        coarse.reshape(-1, count_z), coarse_averaging.T, precision=lax.Precision.HIGHEST
    )
    deepened = deepened.reshape(count_x, 1, count_y, 1, coarse_averaging.shape[0])
    return jnp.broadcast_to(deepened, (count_x, 3, count_y, 3, coarse_averaging.shape[0])).reshape(
        3 * count_x, 3 * count_y, coarse_averaging.shape[0]
    )


def element_contributions(nodal_values, moduli, count_x, count_y, count_z, operator_matrix):
    batch = nodal_values.shape[0]
    corners = []
    for corner in range(8):
        along_x, along_y, along_z = (corner // 4, corner // 2 % 2, corner % 2)
        corners.append(
            nodal_values[
                :,
                :,
                along_x : along_x + count_x,
                along_y : along_y + count_y,
                along_z : along_z + count_z,
            ]
        )
    stacked = jnp.stack(corners, axis=1).reshape(batch, 24, count_x, count_y, count_z)
    product = jnp.einsum(
        "ij,bjxyz->bixyz", operator_matrix, stacked, precision=lax.Precision.HIGHEST
    )
    strain_energy = jnp.sum(stacked * product, axis=1)
    return (strain_energy, moduli[:, None] * product)


def gather_global(external_loads, count_x, count_y, count_z):
    summed = jnp.zeros(
        (external_loads.shape[0], 3, count_x + 1, count_y + 1, count_z + 1), jnp.float32
    )
    for corner in range(8):
        along_x, along_y, along_z = (corner // 4, corner // 2 % 2, corner % 2)
        summed = summed.at[
            :,
            :,
            along_x : along_x + count_x,
            along_y : along_y + count_y,
            along_z : along_z + count_z,
        ].add(external_loads[:, 3 * corner : 3 * corner + 3])
    return summed


def local(design, passive, displacement, support, loading):
    rows_fine, cols_fine, depth_fine = design.shape
    count_x, count_y, count_z = support.shape
    solid_mask = 1.0 - passive.astype(jnp.float32)
    freedom = 1.0 - support.astype(jnp.float32)
    load_values = load_force * loading.astype(jnp.float32)
    start_x = lax.axis_index(WIDE) * rows_fine
    start_y = lax.axis_index(NARROW) * cols_fine
    weights = (
        edge_weights(start_x, rows_fine, rows_fine * lax.axis_size(WIDE))[:, None, None]
        * edge_weights(start_y, cols_fine, cols_fine * lax.axis_size(NARROW))[None, :, None]
        * edge_weights(0, depth_fine, depth_fine)[None, None, :]
    )
    blurred = smooth_field(design) / weights
    coarse_averaging = depth_averaging(depth_fine, count_z)
    densities = []
    slopes = []
    moduli = []
    for level_index in range(3):
        density, slope_term = project(blurred, thresholds[level_index])
        density = density * solid_mask
        densities.append(density)
        slopes.append(slope_term)
        moduli.append(
            aggregate(
                stiff_floor + (1.0 - stiff_floor) * density**3, coarse_averaging, count_x, count_y
            )
        )
    young_modulus = jnp.stack(moduli)
    masked_moves = displacement * freedom
    operator_matrix = jnp.asarray(element_matrix(), dtype=jnp.float32)
    flattened = masked_moves.reshape(9, count_x, count_y, count_z)
    upper_rows = passed_along(flattened[:, :1], WIDE, -1)
    nodal_values = jnp.concatenate([flattened, upper_rows], axis=1)
    upper_cols = passed_along(nodal_values[:, :, :1], NARROW, -1)
    nodal_values = jnp.concatenate([nodal_values, upper_cols], axis=2)
    nodal_values = jnp.pad(nodal_values, ((0, 0), (0, 0), (0, 0), (0, 1))).reshape(
        3, 3, count_x + 1, count_y + 1, count_z + 1
    )
    strain_energy, external_loads = element_contributions(
        nodal_values, young_modulus, count_x, count_y, count_z, operator_matrix
    )
    summed = gather_global(external_loads, count_x, count_y, count_z)
    lower_cols = passed_along(summed[:, :, :, count_y : count_y + 1, :count_z], NARROW, 1)
    summed = summed[:, :, :, :count_y, :count_z].at[:, :, :, :1].add(lower_cols)
    lower_rows = passed_along(summed[:, :, count_x : count_x + 1], WIDE, 1)
    global_gathered = summed[:, :, :count_x].at[:, :, :1].add(lower_rows)
    zeros_field = jnp.zeros_like(load_values)
    applied = jnp.stack([zeros_field, zeros_field, -load_values])
    residual = (applied[None] - global_gathered) * freedom
    partial_sums = jnp.sum(young_modulus * strain_energy, axis=(1, 2, 3))
    compliance = over_axes(partial_sums, WIDE_NARROW)
    gradient = jnp.zeros_like(design)
    for level_index in range(3):
        scaled = strain_energy[level_index] / compliance[level_index]
        gradient = (
            gradient
            - 3.0
            * (1.0 - stiff_floor)
            / 27.0
            * densities[level_index] ** 2
            * spread(scaled, coarse_averaging)
            * slopes[level_index]
            * solid_mask
        )
    sensitivity = smooth_field(gradient / weights)
    return (residual, compliance, sensitivity)


def solution(mesh):
    split = Mesh(
        mesh.devices.reshape(8, 2, 2, 4, 2), ("wide_0", "wide_1", "wide_2", "narrow_0", "narrow_1")
    )
    in_specs = (
        P(WIDE, NARROW, None),
        P(WIDE, NARROW, None),
        P(None, None, WIDE, NARROW, None),
        P(WIDE, NARROW, None),
        P(WIDE, NARROW, None),
    )
    out_specs = (P(None, None, WIDE, NARROW, None), P(), P(WIDE, NARROW, None))
    return jax.shard_map(local, mesh=split, in_specs=in_specs, out_specs=out_specs, check_vma=False)
```

profile of v0, /device:TPU:1, one launch (start us, length us, event | category | flops | bytes accessed | tf_op | source)
XLA Modules:
  0.0 206.6 jit_solution(5248032307218715734)
XLA Ops:
  0.6 1.1 fusion.164
  1.7 4.5 %collective-permute-start = (f32[3,48,384]{2,1,0:T(8,128)S(1)}, f32[3,48,384]{2,1,0:T(8,128)S(1)}, u32[]{:S(2)}, u32[]{:S(2)}) collective-permute-start(f32[3,48,384]{2,1,0:T(8,128)S(1)} %get-tuple-element.143), channel_id=1, source_target_pairs={{0,8},{8,16},{16,24},{24,32},{32,40},{40,48},{48,56},{56,64},{64,7... | collective-permute-start | bytes 663560 | tf_op jit(solution)/shard_map/ppermute | solution.py:31
  6.2 1.9 collective-permute-start.1
  8.9 1.0 broadcast_multiply_fusion
  9.9 1.9 collective-permute-start.4
  12.0 3.6 %collective-permute-done.4 = f32[9,1,16,128]{3,2,1,0:T(8,128)S(1)} collective-permute-done((f32[9,1,16,128]{3,2,1,0:T(8,128)S(1)}, f32[9,1,16,128]{3,2,1,0:T(8,128)S(1)}, u32[]{:S(2)}, u32[]{:S(2)}) %collective-permute-start.4) | collective-permute-done | bytes 73760 | tf_op jit(solution)/shard_map/ppermute | solution.py:40
  15.6 1.3 collective-permute-start.5
  16.9 4.7 %collective-permute-done.5 = f32[9,5,1,128]{3,2,1,0:T(1,128)S(1)} collective-permute-done((f32[9,5,1,128]{3,2,1,0:T(1,128)S(1)}, f32[9,5,1,128]{3,2,1,0:T(1,128)S(1)}, u32[]{:S(2)}, u32[]{:S(2)}) %collective-permute-start.5) | collective-permute-done | bytes 23072 | tf_op jit(solution)/shard_map/ppermute | solution.py:40
  24.2 5.3 %collective-permute-start.2 = (f32[12,3,384]{2,1,0:T(4,128)S(1)}, f32[12,3,384]{2,1,0:T(4,128)S(1)}, u32[]{:S(2)}, u32[]{:S(2)}) collective-permute-start(f32[12,3,384]{2,1,0:T(4,128)S(1)} %get-tuple-element.139), channel_id=1, source_target_pairs={{0,1},{1,2},{2,3},{3,4},{4,5},{5,6},{6,7},{8,9},{9,10},{10,11},{11... | collective-permute-start | bytes 165896 | tf_op jit(solution)/shard_map/ppermute | solution.py:31
  29.5 1.3 collective-permute-start.3
  30.8 4.9 %fusion.1 = f32[3,4,16,128,24]{3,4,2,1,0:T(8,128)} fusion(f32[24,24,1,1,1]{1,0,4,3,2:T(8,128)S(1)} %copy-done.8, f32[3,24,4,16,128]{4,3,2,1,0:T(8,128)S(1)} %bitcast.78), kind=kOutput, calls=%fused_computation.3 | convolution fusion | flops 169869312 | bytes 4720896 | tf_op jit(solution)/shard_map/ij,bjxyz->bixyz/dot_general | solution.py:173
  37.1 2.4 %fusion.43 = (f32[12,48,384]{2,1,0:T(8,128)}, f32[12,48,384]{2,1,0:T(8,128)S(1)}) fusion(s32[12,48,384]{2,1,0:T(8,128)S(1)} %copy-done.1, f32[384]{0:T(512)S(1)} %convert_add_fusion, f32[12,48]{1,0:T(8,128)S(1)} %broadcast_multiply_fusion.1, f32[12,48,384]{2,1,0:T(8,128)S(1)} %fusion.19), kind=kLoop, calls=%fused_computation.95 | loop fusion | flops 5308416 | bytes 3542784 | tf_op jit(solution)/shard_map/add | solution.py:221
  39.5 1.9 fusion.51
  41.4 1.5 dot_general.31
  42.9 2.4 %dot_general.29 = f32[4,3,16,3,384]{4,3,2,1,0:T(4,128)} reshape(f32[12,48,384]{2,1,0:T(8,128)} %get-tuple-element.133) | data formatting | bytes 1769472 | tf_op jit(solution)/shard_map/dot_general | solution.py:138
  45.2 1.2 convolution_reduce_fusion
  46.4 2.5 %convolution_reduce_fusion.1 = f32[4,16,128]{2,1,0:T(8,128)} fusion(f32[4,3,16,3,384]{4,3,2,1,0:T(4,128)} %dot_general.29, s32[384]{0:T(512)S(1)} %add_select_fusion), kind=kOutput, calls=%fused_computation.42 | convolution fusion | flops 339853312 | bytes 919040 | tf_op jit(solution)/shard_map/dot_general | solution.py:138
  48.9 1.5 dot_general.27
  51.8 3.7 %fusion = (f32[3,4,16,128]{3,2,1,0:T(8,128)S(1)}, f32[3,24,4,16,128]{4,3,2,1,0:T(8,128)}) fusion(f32[3,24,4,16,128]{4,3,2,1,0:T(8,128)S(1)} %bitcast.79, f32[3,4,16,128,24]{3,4,2,1,0:T(8,128)} %fusion.1, f32[3,4,16,128]{3,2,1,0:T(8,128)S(1)} %pad_maximum_fusion.6), kind=kLoop, calls=%fused_computation.2 | loop fusion | flops 1744896 | bytes 7274496 | tf_op jit(solution)/shard_map/reduce_sum | solution.py:176
  55.7 16.0 %psum.35 = f32[3]{0:T(128)S(1)} all-reduce(f32[3]{0:T(128)S(1)} %multiply_reduce_fusion), channel_id=1, replica_groups=mesh['wide_0'=8,'wide_1'=2,'wide_2'=2,'narrow_0'=4,'narrow_1'=2] {'wide_0'}, use_global_device_ids=true, to_apply=%region_5.6 | all-reduce | flops 3 | bytes 24 | tf_op jit(solution)/shard_map/psum | solution.py:44
  71.7 3.9 %psum.36 = f32[3]{0:T(128)S(1)} all-reduce(f32[3]{0:T(128)S(1)} %psum.35), channel_id=1, replica_groups=mesh['wide_0'=8,'wide_1'=2,'wide_2'=2,'narrow_0'=4,'narrow_1'=2] {'wide_1'}, use_global_device_ids=true, to_apply=%region_6.7 | all-reduce | flops 3 | bytes 24 | tf_op jit(solution)/shard_map/psum | solution.py:44
  75.6 9.5 %psum.37 = f32[3]{0:T(128)S(1)} all-reduce(f32[3]{0:T(128)S(1)} %psum.36), channel_id=1, replica_groups=mesh['wide_0'=8,'wide_1'=2,'wide_2'=2,'narrow_0'=4,'narrow_1'=2] {'wide_2'}, use_global_device_ids=true, to_apply=%region_7.8 | all-reduce | flops 3 | bytes 24 | tf_op jit(solution)/shard_map/psum | solution.py:44
  85.8 8.7 %psum.38 = f32[3]{0:T(128)S(1)} all-reduce(f32[3]{0:T(128)S(1)} %psum.37), channel_id=1, replica_groups=mesh['wide_0'=8,'wide_1'=2,'wide_2'=2,'narrow_0'=4,'narrow_1'=2] {'narro..., use_global_device_ids=true, to_apply=%region_8.9 | all-reduce | flops 3 | bytes 24 | tf_op jit(solution)/shard_map/psum | solution.py:44
  94.5 1.0 slice.771
  95.5 1.8 fusion.91
  97.4 5.5 %psum.39 = f32[3]{0:T(128)S(1)} all-reduce(f32[3]{0:T(128)S(1)} %psum.38), channel_id=1, replica_groups=mesh['wide_0'=8,'wide_1'=2,'wide_2'=2,'narrow_0'=4,'narrow_1'=2] {'narro..., use_global_device_ids=true, to_apply=%region_9.10 | all-reduce | flops 3 | bytes 24 | tf_op jit(solution)/shard_map/psum | solution.py:44
  104.7 1.4 reshape.821
  106.1 1.0 fusion.108
  107.4 1.4 reshape.819
  108.7 1.0 fusion.110
  109.8 1.2 broadcast_in_dim.9
  111.0 2.5 %reshape.817 = f32[12,48,384]{2,1,0:T(8,128)} reshape(f32[4,3,16,3,384]{4,3,2,1,0:T(4,128)} %broadcast_in_dim.9) | data formatting | bytes 1769472 | tf_op jit(solution)/shard_map/reshape | solution.py:153
  113.5 12.1 %scatter-add.35 = f32[3,3,5,17,129]{4,3,2,1,0:T(8,128)S(1)} dynamic-update-slice(f32[3,3,5,17,129]{4,3,2,1,0:T(8,128)S(1)} %scatter-add.34, f32[3,3,4,16,128]{4,3,2,1,0:T(8,128)} %fusion.91, s32[]{:T(128)} %constant.438.clone.1, s32[]{:T(128)} %constant.438.clone.1, s32[]{:T(128)} %constant.438.clone.1, s32[]{:T(128)} %constant.438.clone.1, s32[]{:T(128)} %constant.442.clone.1) | dynamic-update-slice | bytes 589828 | tf_op jit(solution)/shard_map/scatter-add | solution.py:192
  126.4 2.5 %scatter-add.36 = f32[3,3,5,17,129]{4,3,2,1,0:T(8,128)S(1)} dynamic-update-slice(f32[3,3,5,17,129]{4,3,2,1,0:T(8,128)S(1)} %scatter-add.35, f32[3,3,4,16,128]{4,3,2,1,0:T(8,128)} %slice_add_fusion.6, s32[]{:T(128)} %constant.438.clone.1, s32[]{:T(128)} %constant.438.clone.1, s32[]{:T(128)} %constant.438.clone.1, s32[]{:T(128)} %constant.442.clone.1, s32[]{:T(128)} %constant.438.clone.1) | dynamic-update-slice | bytes 589828 | tf_op jit(solution)/shard_map/scatter-add | solution.py:192
  129.8 12.1 %scatter-add.39 = f32[3,3,5,17,129]{4,3,2,1,0:T(8,128)S(1)} dynamic-update-slice(f32[3,3,5,17,129]{4,3,2,1,0:T(8,128)S(1)} %scatter-add.36, f32[3,3,4,16,128]{4,3,2,1,0:T(8,128)} %slice_add_fusion.5, s32[]{:T(128)} %constant.438.clone.1, s32[]{:T(128)} %constant.438.clone.1, s32[]{:T(128)} %constant.438.clone.1, s32[]{:T(128)} %constant.442.clone.1, s32[]{:T(128)} %constant.442.clone.1) | dynamic-update-slice | bytes 589828 | tf_op jit(solution)/shard_map/scatter-add | solution.py:192
  142.8 12.1 %scatter-add.41 = f32[3,3,5,17,129]{4,3,2,1,0:T(8,128)S(1)} dynamic-update-slice(f32[3,3,5,17,129]{4,3,2,1,0:T(8,128)S(1)} %fusion.92, f32[3,3,4,16,128]{4,3,2,1,0:T(8,128)} %slice_add_fusion.3, s32[]{:T(128)} %constant.438.clone.1, s32[]{:T(128)} %constant.438.clone.1, s32[]{:T(128)} %constant.442.clone.1, s32[]{:T(128)} %constant.438.clone.1, s32[]{:T(128)} %constant.442.clone.1) | dynamic-update-slice | bytes 589828 | tf_op jit(solution)/shard_map/scatter-add | solution.py:192
  155.7 2.5 %scatter-add.44 = f32[3,3,5,17,129]{4,3,2,1,0:T(8,128)S(1)} dynamic-update-slice(f32[3,3,5,17,129]{4,3,2,1,0:T(8,128)S(1)} %scatter-add.41, f32[3,3,4,16,128]{4,3,2,1,0:T(8,128)} %slice_add_fusion.2, s32[]{:T(128)} %constant.438.clone.1, s32[]{:T(128)} %constant.438.clone.1, s32[]{:T(128)} %constant.442.clone.1, s32[]{:T(128)} %constant.442.clone.1, s32[]{:T(128)} %constant.438.clone.1) | dynamic-update-slice | bytes 589828 | tf_op jit(solution)/shard_map/scatter-add | solution.py:192
  159.1 12.1 %scatter-add.45 = f32[3,3,5,17,129]{4,3,2,1,0:T(8,128)S(1)} dynamic-update-slice(f32[3,3,5,17,129]{4,3,2,1,0:T(8,128)S(1)} %scatter-add.44, f32[3,3,4,16,128]{4,3,2,1,0:T(8,128)} %slice_add_fusion.1, s32[]{:T(128)} %constant.438.clone.1, s32[]{:T(128)} %constant.438.clone.1, s32[]{:T(128)} %constant.442.clone.1, s32[]{:T(128)} %constant.442.clone.1, s32[]{:T(128)} %constant.442.clone.1) | dynamic-update-slice | bytes 589828 | tf_op jit(solution)/shard_map/scatter-add | solution.py:192
  171.2 3.2 %collective-permute-start.6 = (f32[3,3,5,1,128]{4,3,2,1,0:T(1,128)S(1)}, f32[3,3,5,1,128]{4,3,2,1,0:T(1,128)S(1)}, u32[]{:S(2)}, u32[]{:S(2)}) collective-permute-start(f32[3,3,5,1,128]{4,3,2,1,0:T(1,128)S(1)} %slice.787), channel_id=1, source_target_pairs={{0,1},{1,2},{2,3},{3,4},{4,5},{5,6},{6,7},{8,9},{9,10},{10,11},{11... | collective-permute-start | bytes 69128 | tf_op jit(solution)/shard_map/ppermute | solution.py:40
  174.4 3.7 %multiply_divide_fusion = f32[12,48,384]{2,1,0:T(8,128)S(1)} fusion(f32[12,48,384]{2,1,0:T(8,128)} %reshape.817, f32[12,48,384]{2,1,0:T(8,128)} %reshape.819, f32[12,48,384]{2,1,0:T(8,128)} %reshape.821, f32[12,48,384]{2,1,0:T(8,128)} %copy-done.2, s32[12,48,384]{2,1,0:T(8,128)} %param.27, f32[384]{0:T(512)S(1)} %convert_add_fusion, ...), kind=kLoop, calls=%fused_computation.35 | loop fusion | flops 10174464 | bytes 5312256 | tf_op jit(solution)/shard_map/div | solution.py:261
  178.3 5.0 %collective-permute-start.7 = (f32[3,3,1,16,128]{4,3,2,1,0:T(8,128)S(1)}, f32[3,3,1,16,128]{4,3,2,1,0:T(8,128)S(1)}, u32[]{:S(2)}, u32[]{:S(2)}) collective-permute-start(f32[3,3,1,16,128]{4,3,2,1,0:T(8,128)S(1)} %slice.790), channel_id=1, source_target_pairs={{0,8},{8,16},{16,24},{24,32},{32,40},{40,48},{48,56},{56,64},{64,7... | collective-permute-start | bytes 221192 | tf_op jit(solution)/shard_map/ppermute | solution.py:40
  183.4 1.9 collective-permute-start.8
  185.3 2.4 %collective-permute-start.9 = (f32[3,48,384]{2,1,0:T(8,128)S(1)}, f32[3,48,384]{2,1,0:T(8,128)S(1)}, u32[]{:S(2)}, u32[]{:S(2)}) collective-permute-start(f32[3,48,384]{2,1,0:T(8,128)S(1)} %get-tuple-element.138), channel_id=1, source_target_pairs={{8,0},{16,8},{24,16},{32,24},{40,32},{48,40},{56,48},{64,56},{72,6... | collective-permute-start | bytes 663560 | tf_op jit(solution)/shard_map/ppermute | solution.py:32
  188.2 4.4 %collective-permute-done.9 = f32[3,48,384]{2,1,0:T(8,128)S(1)} collective-permute-done((f32[3,48,384]{2,1,0:T(8,128)S(1)}, f32[3,48,384]{2,1,0:T(8,128)S(1)}, u32[]{:S(2)}, u32[]{:S(2)}) %collective-permute-start.9) | collective-permute-done | bytes 221216 | tf_op jit(solution)/shard_map/ppermute | solution.py:32
  192.9 4.0 %collective-permute-start.10 = (f32[12,3,384]{2,1,0:T(4,128)S(1)}, f32[12,3,384]{2,1,0:T(4,128)S(1)}, u32[]{:S(2)}, u32[]{:S(2)}) collective-permute-start(f32[12,3,384]{2,1,0:T(4,128)S(1)} %get-tuple-element.135), channel_id=1, source_target_pairs={{0,1},{1,2},{2,3},{3,4},{4,5},{5,6},{6,7},{8,9},{9,10},{10,11},{11... | collective-permute-start | bytes 165896 | tf_op jit(solution)/shard_map/ppermute | solution.py:31
  196.9 1.3 collective-permute-start.11
  199.0 4.5 %collective-permute-done.11 = f32[12,3,384]{2,1,0:T(4,128)S(1)} collective-permute-done((f32[12,3,384]{2,1,0:T(4,128)S(1)}, f32[12,3,384]{2,1,0:T(4,128)S(1)}, u32[]{:S(2)}, u32[]{:S(2)}) %collective-permute-start.11) | collective-permute-done | bytes 55328 | tf_op jit(solution)/shard_map/ppermute | solution.py:32
  204.3 2.3 %fusion.75 = f32[12,48,384]{2,1,0:T(8,128)} fusion(f32[12,48,384]{2,1,0:T(8,128)S(1)} %fusion.6), kind=kLoop, calls=%fused_computation.127 | loop fusion | flops 2433024 | bytes 1769472 | tf_op jit(solution)/shard_map/add | solution.py:96
  (82 shorter events, 15.6 us)
Async XLA Ops:
  1.7 21.0 %collective-permute-start = (f32[3,48,384]{2,1,0:T(8,128)S(1)}, f32[3,48,384]{2,1,0:T(8,128)S(1)}, u32[]{:S(2)}, u32[]{:S(2)}) collective-permute-start(f32[3,48,384]{2,1,0:T(8,128)S(1)} %get-tuple-element.143), channel_id=1, source_target_pairs={{0,8},{8,16},{16,24},{24,32},{32,40},{40,48},{48,56},{56,64},{64,7... | collective-permute-start | bytes 663560 | tf_op jit(solution)/shard_map/ppermute | solution.py:31
  6.2 17.6 %collective-permute-start.1 = (f32[3,48,384]{2,1,0:T(8,128)S(1)}, f32[3,48,384]{2,1,0:T(8,128)S(1)}, u32[]{:S(2)}, u32[]{:S(2)}) collective-permute-start(f32[3,48,384]{2,1,0:T(8,128)S(1)} %get-tuple-element.144), channel_id=1, source_target_pairs={{8,0},{16,8},{24,16},{32,24},{40,32},{48,40},{56,48},{64,56},{72,6... | collective-permute-start | bytes 663560 | tf_op jit(solution)/shard_map/ppermute | solution.py:32
  8.9 1.0 copy-start.5
  9.9 5.7 %collective-permute-start.4 = (f32[9,1,16,128]{3,2,1,0:T(8,128)S(1)}, f32[9,1,16,128]{3,2,1,0:T(8,128)S(1)}, u32[]{:S(2)}, u32[]{:S(2)}) collective-permute-start(f32[9,1,16,128]{3,2,1,0:T(8,128)S(1)} %slice.762), channel_id=1, source_target_pairs={{8,0},{16,8},{24,16},{32,24},{40,32},{48,40},{56,48},{64,56},{72,6... | collective-permute-start | bytes 221192 | tf_op jit(solution)/shard_map/ppermute | solution.py:40
  15.6 6.1 %collective-permute-start.5 = (f32[9,5,1,128]{3,2,1,0:T(1,128)S(1)}, f32[9,5,1,128]{3,2,1,0:T(1,128)S(1)}, u32[]{:S(2)}, u32[]{:S(2)}) collective-permute-start(f32[9,5,1,128]{3,2,1,0:T(1,128)S(1)} %pad_maximum_fusion.7), channel_id=1, source_target_pairs={{1,0},{2,1},{3,2},{4,3},{5,4},{6,5},{7,6},{9,8},{10,9},{11,10},{12... | collective-permute-start | bytes 69128 | tf_op jit(solution)/shard_map/ppermute | solution.py:40
  22.5 1.2 copy-start.3
  23.8 7.0 %copy-start.8 = (f32[24,24,1,1,1]{1,0,4,3,2:T(8,128)S(1)}, f32[24,24,1,1,1]{1,0,4,3,2:T(8,128)}, u32[]{:S(2)}) copy-start(f32[24,24,1,1,1]{1,0,4,3,2:T(8,128)} %constant.477) | copy-start | bytes 6916
  24.2 11.4 %collective-permute-start.2 = (f32[12,3,384]{2,1,0:T(4,128)S(1)}, f32[12,3,384]{2,1,0:T(4,128)S(1)}, u32[]{:S(2)}, u32[]{:S(2)}) collective-permute-start(f32[12,3,384]{2,1,0:T(4,128)S(1)} %get-tuple-element.139), channel_id=1, source_target_pairs={{0,1},{1,2},{2,3},{3,4},{4,5},{5,6},{6,7},{8,9},{9,10},{10,11},{11... | collective-permute-start | bytes 165896 | tf_op jit(solution)/shard_map/ppermute | solution.py:31
  29.5 6.8 %collective-permute-start.3 = (f32[12,3,384]{2,1,0:T(4,128)S(1)}, f32[12,3,384]{2,1,0:T(4,128)S(1)}, u32[]{:S(2)}, u32[]{:S(2)}) collective-permute-start(f32[12,3,384]{2,1,0:T(4,128)S(1)} %get-tuple-element.140), channel_id=1, source_target_pairs={{1,0},{2,1},{3,2},{4,3},{5,4},{6,5},{7,6},{9,8},{10,9},{11,10},{12... | collective-permute-start | bytes 165896 | tf_op jit(solution)/shard_map/ppermute | solution.py:32
  35.7 1.4 copy-start.1
  39.5 1.9 copy-start.2
  51.8 23.8 %copy-start.7 = (s32[4,16,128]{2,1,0:T(8,128)S(1)}, s32[4,16,128]{2,1,0:T(8,128)}, u32[]{:S(2)}) copy-start(s32[4,16,128]{2,1,0:T(8,128)} %param.30) | copy-start | bytes 98308
  102.8 3.3 %copy-start.9 = (f32[3]{0:T(128)}, f32[3]{0:T(128)S(1)}, u32[]{:S(2)}) copy-start(f32[3]{0:T(128)S(1)} %psum.39) | copy-start | bytes 40
  111.0 14.6 %copy-start = (f32[3,24,4,16,128]{4,3,2,1,0:T(8,128)S(1)}, f32[3,24,4,16,128]{4,3,2,1,0:T(8,128)}, u32[]{:S(2)}) copy-start(f32[3,24,4,16,128]{4,3,2,1,0:T(8,128)} %get-tuple-element.132) | copy-start | bytes 7077892
  171.2 6.9 %collective-permute-start.6 = (f32[3,3,5,1,128]{4,3,2,1,0:T(1,128)S(1)}, f32[3,3,5,1,128]{4,3,2,1,0:T(1,128)S(1)}, u32[]{:S(2)}, u32[]{:S(2)}) collective-permute-start(f32[3,3,5,1,128]{4,3,2,1,0:T(1,128)S(1)} %slice.787), channel_id=1, source_target_pairs={{0,1},{1,2},{2,3},{3,4},{4,5},{5,6},{6,7},{8,9},{9,10},{10,11},{11... | collective-permute-start | bytes 69128 | tf_op jit(solution)/shard_map/ppermute | solution.py:40
  178.3 9.4 %collective-permute-start.7 = (f32[3,3,1,16,128]{4,3,2,1,0:T(8,128)S(1)}, f32[3,3,1,16,128]{4,3,2,1,0:T(8,128)S(1)}, u32[]{:S(2)}, u32[]{:S(2)}) collective-permute-start(f32[3,3,1,16,128]{4,3,2,1,0:T(8,128)S(1)} %slice.790), channel_id=1, source_target_pairs={{0,8},{8,16},{16,24},{24,32},{32,40},{40,48},{48,56},{56,64},{64,7... | collective-permute-start | bytes 221192 | tf_op jit(solution)/shard_map/ppermute | solution.py:40
  183.4 4.8 %collective-permute-start.8 = (f32[3,48,384]{2,1,0:T(8,128)S(1)}, f32[3,48,384]{2,1,0:T(8,128)S(1)}, u32[]{:S(2)}, u32[]{:S(2)}) collective-permute-start(f32[3,48,384]{2,1,0:T(8,128)S(1)} %get-tuple-element.137), channel_id=1, source_target_pairs={{0,8},{8,16},{16,24},{24,32},{32,40},{40,48},{48,56},{56,64},{64,7... | collective-permute-start | bytes 663560 | tf_op jit(solution)/shard_map/ppermute | solution.py:31
  185.3 7.3 %collective-permute-start.9 = (f32[3,48,384]{2,1,0:T(8,128)S(1)}, f32[3,48,384]{2,1,0:T(8,128)S(1)}, u32[]{:S(2)}, u32[]{:S(2)}) collective-permute-start(f32[3,48,384]{2,1,0:T(8,128)S(1)} %get-tuple-element.138), channel_id=1, source_target_pairs={{8,0},{16,8},{24,16},{32,24},{40,32},{48,40},{56,48},{64,56},{72,6... | collective-permute-start | bytes 663560 | tf_op jit(solution)/shard_map/ppermute | solution.py:32
  187.8 10.4 %copy-start.4 = (f32[3,4,16,128]{3,2,1,0:T(8,128)S(1)}, f32[3,4,16,128]{3,2,1,0:T(8,128)}, u32[]{:S(2)}) copy-start(f32[3,4,16,128]{3,2,1,0:T(8,128)} %stack.41) | copy-start | bytes 294916
  187.8 10.4 %copy-start.6 = (f32[4,16,128]{2,1,0:T(8,128)S(1)}, f32[4,16,128]{2,1,0:T(8,128)}, u32[]{:S(2)}) copy-start(f32[4,16,128]{2,1,0:T(8,128)} %copy-done.5) | copy-start | bytes 98308
  192.9 6.1 %collective-permute-start.10 = (f32[12,3,384]{2,1,0:T(4,128)S(1)}, f32[12,3,384]{2,1,0:T(4,128)S(1)}, u32[]{:S(2)}, u32[]{:S(2)}) collective-permute-start(f32[12,3,384]{2,1,0:T(4,128)S(1)} %get-tuple-element.135), channel_id=1, source_target_pairs={{0,1},{1,2},{2,3},{3,4},{4,5},{5,6},{6,7},{8,9},{9,10},{10,11},{11... | collective-permute-start | bytes 165896 | tf_op jit(solution)/shard_map/ppermute | solution.py:31
  196.9 6.6 %collective-permute-start.11 = (f32[12,3,384]{2,1,0:T(4,128)S(1)}, f32[12,3,384]{2,1,0:T(4,128)S(1)}, u32[]{:S(2)}, u32[]{:S(2)}) collective-permute-start(f32[12,3,384]{2,1,0:T(4,128)S(1)} %get-tuple-element.136), channel_id=1, source_target_pairs={{1,0},{2,1},{3,2},{4,3},{5,4},{6,5},{7,6},{9,8},{10,9},{11,10},{12... | collective-permute-start | bytes 165896 | tf_op jit(solution)/shard_map/ppermute | solution.py:32
where the time goes:
time: 208 us; the launch traced here: 207 us
  local copies, waits for them, and re-layouts  71.5 us (34%)
  blocking collectives  43.6 us (21%)
  starting transfers between devices  34 us (16%)
  other arithmetic  25.9 us (12%)
  waiting for transfers between devices  18.2 us (9%)
  matrix products  12.1 us (6%)
    scatter-add x7, local copies, waits for them, and re-layouts, gather_global(): summed = summed.at[:, :, along_x:along_x + count_x, along_y:along_y + cou...  53.5 us
    psum x5, blocking collectives, over_axes(): return functools.reduce(lax.psum, axes, shard)  43.6 us
    ppermute x4, starting transfers between devices, with_halo(): before = lax.ppermute(last, axis, up)  15.7 us
    ppermute x4, starting transfers between devices, passed_along(): return lax.ppermute(block, axis, route)  11.4 us
    ppermute x4, waiting for transfers between devices, with_halo(): after = lax.ppermute(initial, axis, down)  9.53 us
    ppermute x4, waiting for transfers between devices, passed_along(): return lax.ppermute(block, axis, route)  8.35 us
    ppermute x4, starting transfers between devices, with_halo(): after = lax.ppermute(initial, axis, down)  6.92 us
    add x6, other arithmetic, gather_global(): summed = summed.at[:, :, along_x:along_x + count_x, along_y:along_y + cou...  5.98 us
  transfers between devices with their start and end apart: 12, of which 6 were waited for; matrix products, arithmetic and copies ran while one was open for 6% of the time, Pallas kernels for 0%

commit v1 on v0

v1 whole, which is shorter than its diff:
```python
import functools
import math

import jax
import jax.numpy as jnp
import numpy as np
from jax import lax
from jax.experimental import pallas as pl
from jax.experimental.pallas import tpu as pltpu
from jax.sharding import PartitionSpec as P

sharpness = 8.0
thresholds = (0.7, 0.5, 0.3)
stiff_floor = 0.001
load_force = 4.0
poisson = 0.3

F32, BF16 = jnp.float32, jnp.bfloat16
MESH = pl.DeviceIdType.MESH
ROWS, COLS, DEEP = 12, 48, 384
EX, EY, EZ = 4, 16, 128
DIRS = ((1, 0), (-1, 0), (0, 1), (0, -1), (1, 1), (1, -1), (-1, 1), (-1, -1))


def element_matrix():
    inv_root = 1.0 / np.sqrt(3.0)
    elastic = np.full((3, 3), poisson) + np.eye(3) * (1.0 - 2.0 * poisson)
    elastic = np.block(
        [[elastic, np.zeros((3, 3))], [np.zeros((3, 3)), np.eye(3) * (0.5 - poisson)]]
    ) / ((1.0 + poisson) * (1.0 - 2.0 * poisson))
    signs = [(2 * (c // 4) - 1, 2 * (c // 2 % 2) - 1, 2 * (c % 2) - 1) for c in range(8)]
    stiffness = np.zeros((24, 24))
    for ga in (-inv_root, inv_root):
        for gb in (-inv_root, inv_root):
            for gc in (-inv_root, inv_root):
                point = (ga, gb, gc)
                strain = np.zeros((6, 24))
                for c in range(8):
                    d = []
                    for along in range(3):
                        s = signs[c][along] / 4.0
                        for other in range(3):
                            if other != along:
                                s = s * (1.0 + signs[c][other] * point[other])
                        d.append(s)
                    col = 3 * c
                    strain[0, col], strain[1, col + 1], strain[2, col + 2] = d
                    strain[3, col], strain[3, col + 1] = d[1], d[0]
                    strain[4, col + 1], strain[4, col + 2] = d[2], d[1]
                    strain[5, col], strain[5, col + 2] = d[2], d[0]
                stiffness = stiffness + strain.T @ elastic @ strain * 0.125
    return stiffness


def mode_matrix():
    h = np.zeros((8, 8))
    for mode in range(8):
        for c in range(8):
            v = 1.0
            for bit in (4, 2, 1):
                if mode & bit:
                    v *= 1.0 if c & bit else -1.0
            h[mode, c] = v
    full = np.kron(h, np.eye(3))
    k = full @ element_matrix() @ full.T / 64.0
    return [
        [(j, float(k[i, j])) for j in range(24) if abs(k[i, j]) > 1e-9] for i in range(24)
    ]


def tent(values):
    p = [a + b for a, b in zip(values, values[1:])]
    q = [a + b for a, b in zip(p, p[2:])]
    r = [a + b for a, b in zip(q, q[1:])]
    return [a + b for a, b in zip(r, r[2:])]


def inverse_weight(place, extent):
    edge = jnp.minimum(place, extent - 1 - place)
    return jnp.where(
        edge >= 3, 1.0 / 16.0, jnp.where(edge == 2, 1.0 / 15.0, jnp.where(edge == 1, 1.0 / 13.0, 0.1))
    ).astype(F32)


def split(value):
    high = value.astype(BF16)
    return high, (value - high.astype(F32)).astype(BF16)


def times(value, matrix):
    high, low = split(value)
    return jnp.dot(high, matrix, preferred_element_type=F32) + jnp.dot(
        low, matrix, preferred_element_type=F32
    )


def level(bl, eta):
    low = math.tanh(sharpness * eta)
    den = low + math.tanh(sharpness * (1.0 - eta))
    t = jnp.tanh(bl * sharpness - sharpness * eta)
    rho = t * (1.0 / den) + low / den
    return rho, 1.0 - t * t


def slope_scale(eta):
    den = math.tanh(sharpness * eta) + math.tanh(sharpness * (1.0 - eta))
    return sharpness / den * 3.0 * (1.0 - stiff_floor) / 27.0


def kernel(
    wide, narrow,
    design, passive, disp, support, loading,
    res_out, comp_out, sens_out,
    D, XF, AH, AL, PA, BL, T, EN, ESP, GX, OUT, V, M, FS, FXR, FYR, FDR, U, SU, LO, RES, MOD, S3,
    WT, BAND, SPREAD, GATHER, AR1, AR2, RX,
    lsem, osem, dss, drs, mss, mrs, bss, brs, ess, ers, fss, frs, a1s, a1r, a2s, a2r,
):
    w = lax.axis_index("wide")
    n = lax.axis_index("narrow")
    zc, xl, core = w // 4, (w // 2) % 2, w % 2
    count1, count2 = wide // 2, 2 * narrow
    i1 = zc * 2 + core
    i2 = xl * narrow + n

    def within(dw, dn):
        ok = None
        for step, at, count in ((dw, w, wide), (dn, n, narrow)):
            if step:
                cond = at < count - 1 if step > 0 else at > 0
                ok = cond if ok is None else ok & cond
        return ok

    def peer1(k):
        j = (i1 + k) % count1
        return j, ((j // 2) * 4 + xl * 2 + j % 2, n)

    def peer2(k):
        j = (i2 + k) % count2
        return j, (zc * 4 + (j // narrow) * 2 + core, j % narrow)

    def around(dw, dn):
        return ((w + dw + wide) % wide, (n + dn + narrow) % narrow)

    barrier = pltpu.get_barrier_semaphore()
    total = count1 - 1 + count2 - 1
    for dw, dn in DIRS:
        total = total + within(dw, dn).astype(jnp.int32)

        @pl.when(within(dw, dn))
        def _(dw=dw, dn=dn):
            pl.semaphore_signal(barrier, 1, device_id=around(dw, dn), device_id_type=MESH)

    for k in range(1, count1):
        pl.semaphore_signal(barrier, 1, device_id=peer1(k)[1], device_id_type=MESH)
    for k in range(1, count2):
        pl.semaphore_signal(barrier, 1, device_id=peer2(k)[1], device_id_type=MESH)

    loads = [
        pltpu.make_async_copy(disp, U, lsem.at[0]),
        pltpu.make_async_copy(support, SU, lsem.at[1]),
        pltpu.make_async_copy(design, D.at[3:15, 8:56, :], lsem.at[2]),
        pltpu.make_async_copy(loading, LO, lsem.at[3]),
    ] + [
        pltpu.make_async_copy(passive.at[:, :, 128 * c : 128 * c + 128], PA.at[:, c], lsem.at[4 + c])
        for c in range(3)
    ]
    for copy in loads:
        copy.start()

    def near(shape):
        return lax.broadcasted_iota(jnp.int32, shape, 0), lax.broadcasted_iota(jnp.int32, shape, 1)

    a, b = near((DEEP, DEEP))
    BAND[...] = jnp.maximum(4 - jnp.abs(a - b), 0).astype(F32).astype(BF16)
    a, b = near((EZ, DEEP))
    gap = b - 3 * a
    SPREAD[...] = jnp.where((gap >= 0) & (gap < 3), 1.0, 0.0).astype(BF16)
    a, b = near((DEEP, EZ))
    gap = a - 3 * b
    GATHER[...] = jnp.where((gap >= 0) & (gap < 3), 1.0, 0.0).astype(BF16)
    a, b = near((24, DEEP))
    a = jnp.where(a == 23, -1, a)
    deep = inverse_weight(b, DEEP)
    for m in range(3):
        WT[m] = inverse_weight(n * COLS + 3 * a + m, narrow * COLS) * deep
    for x in range(18):
        RX[x] = inverse_weight(w * ROWS + x - 3, wide * ROWS)

    zero = functools.partial(jnp.zeros, dtype=F32)

    @pl.when(w == 0)
    def _():
        D[0:3] = zero((3, 64, DEEP))
        BL[0:3] = zero((3, 3, 32, DEEP))
        EN[:, 0] = zero((3, 32, 128))
        FXR[...] = zero((9, 16, 128))

    @pl.when(w == wide - 1)
    def _():
        D[15:18] = zero((3, 64, DEEP))
        BL[15:18] = zero((3, 3, 32, DEEP))
        EN[:, 5] = zero((3, 32, 128))
        M[:, 4] = zero((9, 24, 128))

    @pl.when(n == 0)
    def _():
        D[:, 0:8] = zero((18, 8, DEEP))
        BL[:, :, 0:8] = zero((18, 3, 8, DEEP))
        EN[:, :, 0:8] = zero((3, 6, 8, 128))
        FYR[...] = zero((9, 4, 8, 128))

    @pl.when(n == narrow - 1)
    def _():
        D[:, 56:64] = zero((18, 8, DEEP))
        BL[:, :, 24:32] = zero((18, 3, 8, DEEP))
        EN[:, :, 24:32] = zero((3, 6, 8, 128))
        M[:, :, 16:24] = zero((9, 5, 8, 128))

    @pl.when((n == 0) | (w == 0))
    def _():
        FDR[...] = zero((9, 8, 128))

    FS[...] = zero((9, 5, 24, 128))

    class Message:
        def __init__(self, src, dst, ss, rs, dw, dn):
            self.to, self.origin = within(dw, dn), within(-dw, -dn)
            self.copy = pltpu.make_async_remote_copy(
                src_ref=src, dst_ref=dst, send_sem=ss, recv_sem=rs,
                device_id=around(dw, dn), device_id_type=MESH,
            )

        def start(self):
            pl.when(self.to)(self.copy.start)

        def wait_send(self):
            pl.when(self.to)(self.copy.wait_send)

        def wait_recv(self):
            pl.when(self.origin)(self.copy.wait_recv)

    def x_part(dw, low, high, depth):
        if dw == 0:
            return pl.ds(low, high - low), pl.ds(low, high - low)
        if dw > 0:
            return pl.ds(high - depth, depth), pl.ds(low - depth, depth)
        return pl.ds(low, depth), pl.ds(high, depth)

    designs, fields, energies = [], [], []
    for d, (dw, dn) in enumerate(DIRS):
        sx, tx = x_part(dw, 0, ROWS, 3)
        tx = pl.ds(tx.start + 3, tx.size)
        sy, ty = x_part(dn, 0, COLS, 3)
        ty = pl.ds(ty.start + 8, ty.size)
        designs.append(
            Message(design.at[sx, sy, :], D.at[tx, ty, :], dss.at[d], drs.at[d], dw, dn)
        )
        sx, tx = x_part(dw, 3, 15, 3)
        sy, ty = x_part(dn, 8, 24, 1)
        fields.append(
            Message(BL.at[sx, :, sy, :], BL.at[tx, :, ty, :], bss.at[d], brs.at[d], dw, dn)
        )
        sx, tx = x_part(dw, 1, 5, 1)
        energies.append(
            Message(EN.at[:, sx, sy, :], EN.at[:, tx, ty, :], ess.at[d], ers.at[d], dw, dn)
        )
    moves, forces = [], []
    for d, (dw, dn) in enumerate(((-1, 0), (0, -1), (-1, -1))):
        sx, tx = x_part(dw, 0, 4, 1)
        sy, ty = x_part(dn, 0, 16, 1)
        moves.append(Message(M.at[:, sx, sy, :], M.at[:, tx, ty, :], mss.at[d], mrs.at[d], dw, dn))
    forces.append(Message(FS.at[:, 4, 0:16, :], FXR, fss.at[0], frs.at[0], 1, 0))
    forces.append(
        Message(FS.at[:, 0:4, 16:17, :], FYR.at[:, :, 0:1, :], fss.at[1], frs.at[1], 0, 1)
    )
    forces.append(Message(FS.at[:, 4, 16:17, :], FDR.at[:, 0:1, :], fss.at[2], frs.at[2], 1, 1))

    loads[0].wait()
    loads[1].wait()
    free = 1.0 - SU[...].astype(F32)
    for k in range(9):
        M[k, 0:4, 0:16] = U[k] * free

    pl.semaphore_wait(barrier, total)
    for message in moves:
        message.start()
    for message in designs:
        message.start()

    modes = mode_matrix()
    lane = lax.broadcasted_iota(jnp.int32, (8, 128), 1)
    for message in moves:
        message.wait_recv()

    def energy_step(i, _):
        r, l = i // 4, i % 4
        for t in range(2):
            hat = [None] * 24
            for comp in range(3):
                k = r * 3 + comp
                corner = {}
                for p in range(2):
                    for q in range(2):
                        v = M[k, l + p, pl.ds(8 * t + q, 8), :]
                        v1 = jnp.where(lane < 127, pltpu.roll(v, 127, axis=1), 0.0)
                        corner[p, q, 0], corner[p, q, 1] = v + v1, v1 - v
                for s in range(2):
                    y = {}
                    for p in range(2):
                        y[p, 0] = corner[p, 0, s] + corner[p, 1, s]
                        y[p, 1] = corner[p, 1, s] - corner[p, 0, s]
                    for q in range(2):
                        hat[3 * (2 * q + s) + comp] = y[0, q] + y[1, q]
                        hat[3 * (4 + 2 * q + s) + comp] = y[1, q] - y[0, q]
            energy = None
            for row in range(24):
                if not modes[row]:
                    continue
                value = None
                for j, factor in modes[row]:
                    term = hat[j] * factor
                    value = term if value is None else value + term
                V[i, row, 8 * t : 8 * t + 8] = value
                term = value * hat[row]
                energy = term if energy is None else energy + term
            EN[r, 1 + l, 8 + 8 * t : 16 + 8 * t] = energy
        return 0

    lax.fori_loop(0, 12, energy_step, 0)
    for message in energies:
        message.start()

    loads[2].wait()
    for message in designs:
        message.wait_recv()

    def x_step(t, _):
        rows = pl.ds(pl.multiple_of(8 * t, 8), 8)
        for c in range(3):
            out = tent([D[x, rows, 128 * c : 128 * c + 128] for x in range(18)])
            for x in range(ROWS):
                XF[x, c, rows, :] = out[x]
        return 0

    lax.fori_loop(0, 8, x_step, 0)

    def keep(x, parts):
        for m in range(3):
            block = jnp.concatenate(
                [jnp.concatenate([parts[m, t, c] for t in range(2)], axis=0) for c in range(3)], axis=1
            )
            high, low = split(block)
            AH[x, 16 * m : 16 * m + 16, :] = high
            AL[x, 16 * m : 16 * m + 16, :] = low

    def y_step(x, _):
        parts = {}
        for t in range(2):
            for c in range(3):
                out = tent([XF[x, c, pl.ds(8 + 24 * t + k, 8, stride=3), :] for k in range(-3, 6)])
                for m in range(3):
                    parts[m, t, c] = out[m]
        keep(x, parts)
        return 0

    lax.fori_loop(0, ROWS, y_step, 0)
    for copy in loads[4:]:
        copy.wait()

    def banded(g):
        rows = pl.ds(3 * g, 3)
        band = BAND[...]
        return jnp.dot(
            AH[rows].reshape(144, DEEP), band, preferred_element_type=F32
        ) + jnp.dot(AL[rows].reshape(144, DEEP), band, preferred_element_type=F32)

    def z_step(g, _):
        z = banded(g)
        for xr in range(3):
            x = 3 * g + xr
            for m in range(3):
                value = z[16 * (3 * xr + m) : 16 * (3 * xr + m) + 16] * (WT[m, 0:16] * RX[x + 3])
                for t in range(2):
                    for c in range(3):
                        void = PA[x, c, pl.ds(24 * t + m, 8, stride=3), :]
                        part = value[8 * t : 8 * t + 8, 128 * c : 128 * c + 128]
                        BL[x + 3, m, 8 + 8 * t : 16 + 8 * t, 128 * c : 128 * c + 128] = part * (
                            1.0 - void.astype(F32)
                        )
        return 0

    lax.fori_loop(0, 4, z_step, 0)
    for message in fields:
        message.start()

    def own_step(xe, _):
        sums = [None] * 3
        for xr in range(3):
            for m in range(3):
                bl = BL[3 + 3 * xe + xr, m, 8:24, :]
                for r in range(3):
                    rho, slope = level(bl, thresholds[r])
                    square = rho * rho
                    T[r, 3 + 3 * xe + xr, m, 0:16] = square * slope
                    cube = square * rho
                    sums[r] = cube if sums[r] is None else sums[r] + cube
        for r in range(3):
            S3[r, xe] = sums[r]
        return 0

    lax.fori_loop(0, 4, own_step, 0)
    moduli = times(S3[...].reshape(192, DEEP), GATHER[...]) * ((1.0 - stiff_floor) / 27.0) + stiff_floor
    MOD[...] = moduli.reshape(12, 16, 128)
    row8 = lax.broadcasted_iota(jnp.int32, (8, 128), 0)
    tile = zero((8, 128))
    for r in range(3):
        part = zero((8, 128))
        for l in range(4):
            for t in range(2):
                part = part + MOD[4 * r + l, 8 * t : 8 * t + 8] * EN[r, 1 + l, 8 + 8 * t : 16 + 8 * t]
        tile = jnp.where(row8 == r, jnp.sum(part, axis=0, keepdims=True), tile)
    AR1[i1] = tile

    def exchange(buf, ss, rs, me, count, peer):
        out = []
        for k in range(1, count):
            j, device = peer(k)
            send = pltpu.make_async_remote_copy(
                src_ref=buf.at[me], dst_ref=buf.at[me], send_sem=ss.at[k], recv_sem=rs.at[me],
                device_id=device, device_id_type=MESH,
            )
            recv = pltpu.make_async_remote_copy(
                src_ref=buf.at[j], dst_ref=buf.at[j], send_sem=ss.at[k], recv_sem=rs.at[j],
                device_id=device, device_id_type=MESH,
            )
            out.append((send, recv))
        return out

    phase1 = exchange(AR1, a1s, a1r, i1, count1, peer1)
    phase2 = exchange(AR2, a2s, a2r, i2, count2, peer2)
    for send, _ in phase1:
        send.start()

    def force_step(i, _):
        r, l = i // 4, i % 4
        for t in range(2):
            mod = MOD[i, 8 * t : 8 * t + 8]
            for comp in range(3):
                k = r * 3 + comp

                def mode(p, q, s):
                    row = 3 * (4 * p + 2 * q + s) + comp
                    return V[i, row, 8 * t : 8 * t + 8] * mod if modes[row] else None

                def minus(a, b):
                    return b * -1.0 if a is None else a - b

                def plus(a, b):
                    return b if a is None else a + b

                zz = {}
                for p in range(2):
                    for q in range(2):
                        v0, v1 = mode(p, q, 0), mode(p, q, 1)
                        high = jnp.where(lane > 0, pltpu.roll(plus(v0, v1), 1, axis=1), 0.0)
                        zz[p, q] = minus(v0, v1) + high
                for c in range(2):
                    y0, y1 = [
                        (zz[p, 1] + zz[p, 0]) if c else (zz[p, 0] - zz[p, 1]) for p in range(2)
                    ]
                    rows = pl.ds(8 * t + c, 8)
                    FS[k, l, rows, :] = FS[k, l, rows, :] + (y0 - y1)
                    FS[k, l + 1, rows, :] = FS[k, l + 1, rows, :] + (y0 + y1)
        return 0

    lax.fori_loop(0, 12, force_step, 0)
    for message in forces:
        message.start()

    for _, recv in phase1:
        recv.wait_recv()
    total1 = AR1[0]
    for j in range(1, count1):
        total1 = total1 + AR1[j]
    AR2[i2] = total1
    for send, _ in phase2:
        send.start()

    for message in energies:
        message.wait_recv()
    for r in range(3):
        for l in range(6):
            edge = jnp.where(row8 == 7, EN[r, l, 0:8], EN[r, l, 24:32])
            block = jnp.concatenate([EN[r, l, 8:24], edge], axis=0)
            ESP[r, l] = times(block, SPREAD[...])

    def own_terms(xe, _):
        for xr in range(3):
            x = 3 + 3 * xe + xr
            for m in range(3):
                scale = WT[m, 0:16] * RX[x]
                for r in range(3):
                    T[r, x, m, 0:16] = T[r, x, m, 0:16] * (ESP[r, 1 + xe, 0:16] * scale)
        return 0

    lax.fori_loop(0, 4, own_terms, 0)
    for message in fields:
        message.wait_recv()

    def terms(x, xe, m, bl, rows):
        scale = WT[m, rows] * RX[x]
        for r in range(3):
            rho, slope = level(bl, thresholds[r])
            T[r, x, m, rows] = rho * rho * slope * (ESP[r, xe, rows] * scale)

    for l in (0, 5):

        def row_terms(xr, _, l=l):
            for m in range(3):
                terms(3 * l + xr, l, m, BL[3 * l + xr, m, 8:24, :], slice(0, 16))
            return 0

        lax.fori_loop(0, 3, row_terms, 0)

    def column_terms(x, _):
        for m in range(3):
            edge = lax.broadcasted_iota(jnp.int32, (8, DEEP), 0) == 7
            bl = jnp.where(edge, BL[x, m, 0:8, :], BL[x, m, 24:32, :])
            terms(x, x // 3, m, bl, slice(16, 24))
        return 0

    lax.fori_loop(0, 18, column_terms, 0)

    for message in forces:
        message.wait_recv()
    loads[3].wait()
    for k in range(9):
        FS[k, 0, 0:16] = FS[k, 0, 0:16] + FXR[k]
        FS[k, 0:4, 0:8] = FS[k, 0:4, 0:8] + jnp.where(
            lax.broadcasted_iota(jnp.int32, (4, 8, 128), 1) == 0, FYR[k], 0.0
        )
        FS[k, 0, 0:8] = FS[k, 0, 0:8] + jnp.where(row8 == 0, FDR[k], 0.0)
    free = 1.0 - SU[...].astype(F32)
    load = LO[...].astype(F32) * (-load_force)
    for k in range(9):
        stiff = FS[k, 0:4, 0:16]
        RES[k] = ((load - stiff) if k % 3 == 2 else (0.0 - stiff)) * free
    res_copy = pltpu.make_async_copy(RES, res_out, osem.at[12])
    res_copy.start()

    for _, recv in phase2:
        recv.wait_recv()
    total2 = AR2[0]
    for j in range(1, count2):
        total2 = total2 + AR2[j]
    scales = []
    for r in range(3):
        comp_out[r] = jnp.sum(total2[r : r + 1])
        whole = jnp.sum(total2[r : r + 1], axis=1, keepdims=True)
        scales.append(jnp.broadcast_to(-slope_scale(thresholds[r]) / whole, (8, 128)))

    def x_back(m, _):
        for t in range(3):
            for c in range(3):
                lanes = slice(128 * c, 128 * c + 128)
                rows = slice(8 * t, 8 * t + 8)
                values = []
                for x in range(18):
                    v = T[0, x, m, rows, lanes] * scales[0]
                    v = v + T[1, x, m, rows, lanes] * scales[1]
                    values.append(v + T[2, x, m, rows, lanes] * scales[2])
                out = tent(values)
                for x in range(ROWS):
                    GX[x, m, c, 8 + 8 * t : 16 + 8 * t, :] = out[x]
                    if t == 2:
                        GX[x, m, c, 0:8, :] = out[x]
        return 0

    lax.fori_loop(0, 3, x_back, 0)

    def y_back(x, _):
        parts = {}
        for t in range(2):
            for c in range(3):
                out = tent([GX[x, k % 3, c, pl.ds(8 + 8 * t + k // 3, 8), :] for k in range(-3, 6)])
                for m in range(3):
                    parts[m, t, c] = out[m]
        keep(x, parts)
        return 0

    lax.fori_loop(0, ROWS, y_back, 0)

    def out_copy(g, c):
        return pltpu.make_async_copy(
            OUT.at[pl.ds(3 * g, 3), c],
            sens_out.at[pl.ds(3 * g, 3), :, 128 * c : 128 * c + 128],
            osem.at[3 * g + c],
        )

    def z_back(g, _):
        z = banded(g)
        for xr in range(3):
            for m in range(3):
                for t in range(2):
                    for c in range(3):
                        at = 16 * (3 * xr + m) + 8 * t
                        OUT[3 * g + xr, c, pl.ds(24 * t + m, 8, stride=3), :] = z[
                            at : at + 8, 128 * c : 128 * c + 128
                        ]
        for c in range(3):
            out_copy(g, c).start()
        return 0

    lax.fori_loop(0, 4, z_back, 0)

    for message in designs + moves + fields + energies + forces:
        message.wait_send()
    for send, _ in phase1 + phase2:
        send.wait_send()
    res_copy.wait()
    for g in range(4):
        for c in range(3):
            out_copy(g, c).wait()


def solution(mesh):
    wide, narrow = mesh.shape["wide"], mesh.shape["narrow"]

    def local(design, passive, displacement, support, loading):
        sems = pltpu.SemaphoreType.DMA
        residual, compliance, sensitivity = pl.pallas_call(
            functools.partial(kernel, wide, narrow),
            out_shape=(
                jax.ShapeDtypeStruct((9, EX, EY, EZ), F32),
                jax.ShapeDtypeStruct((3,), F32),
                jax.ShapeDtypeStruct((ROWS, COLS, DEEP), F32),
            ),
            in_specs=[pl.BlockSpec(memory_space=pl.ANY)] * 5,
            out_specs=(
                pl.BlockSpec(memory_space=pl.ANY),
                pl.BlockSpec(memory_space=pltpu.SMEM),
                pl.BlockSpec(memory_space=pl.ANY),
            ),
            scratch_shapes=[
                pltpu.VMEM((18, 64, DEEP), F32),
                pltpu.VMEM((ROWS, 3, 64, 128), F32),
                pltpu.VMEM((ROWS, COLS, DEEP), BF16),
                pltpu.VMEM((ROWS, COLS, DEEP), BF16),
                pltpu.VMEM((ROWS, 3, COLS, 128), jnp.int32),
                pltpu.VMEM((18, 3, 32, DEEP), F32),
                pltpu.VMEM((3, 18, 3, 24, DEEP), F32),
                pltpu.VMEM((3, 6, 32, 128), F32),
                pltpu.VMEM((3, 6, 24, DEEP), F32),
                pltpu.VMEM((ROWS, 3, 3, 32, 128), F32),
                pltpu.VMEM((ROWS, 3, COLS, 128), F32),
                pltpu.VMEM((12, 24, 16, 128), F32),
                pltpu.VMEM((9, 5, 24, 128), F32),
                pltpu.VMEM((9, 5, 24, 128), F32),
                pltpu.VMEM((9, 16, 128), F32),
                pltpu.VMEM((9, 4, 8, 128), F32),
                pltpu.VMEM((9, 8, 128), F32),
                pltpu.VMEM((9, EX, EY, EZ), F32),
                pltpu.VMEM((EX, EY, EZ), jnp.int32),
                pltpu.VMEM((EX, EY, EZ), jnp.int32),
                pltpu.VMEM((9, EX, EY, EZ), F32),
                pltpu.VMEM((12, 16, 128), F32),
                pltpu.VMEM((3, 4, 16, DEEP), F32),
                pltpu.VMEM((3, 24, DEEP), F32),
                pltpu.VMEM((DEEP, DEEP), BF16),
                pltpu.VMEM((EZ, DEEP), BF16),
                pltpu.VMEM((DEEP, EZ), BF16),
                pltpu.VMEM((wide // 2, 8, 128), F32),
                pltpu.VMEM((2 * narrow, 8, 128), F32),
                pltpu.SMEM((18,), F32),
                sems((7,)), sems((13,)),
                sems((8,)), sems((8,)), sems((3,)), sems((3,)), sems((8,)), sems((8,)),
                sems((8,)), sems((8,)), sems((3,)), sems((3,)),
                sems((wide // 2,)), sems((wide // 2,)), sems((2 * narrow,)), sems((2 * narrow,)),
            ],
            compiler_params=pltpu.CompilerParams(
                collective_id=0, has_side_effects=True, vmem_limit_bytes=56 << 20
            ),
        )(design, passive, displacement.reshape(9, EX, EY, EZ), support, loading)
        return residual.reshape(3, 3, EX, EY, EZ), compliance, sensitivity

    in_specs = (
        P("wide", "narrow", None),
        P("wide", "narrow", None),
        P(None, None, "wide", "narrow", None),
        P("wide", "narrow", None),
        P("wide", "narrow", None),
    )
    out_specs = (P(None, None, "wide", "narrow", None), P(), P("wide", "narrow", None))
    return jax.shard_map(local, mesh=mesh, in_specs=in_specs, out_specs=out_specs, check_vma=False)
```

time: 208 us -> 47.6 us (0.23)
  local copies, waits for them, and re-layouts: 71.5 us -> 4.35 us
  blocking collectives: 43.6 us -> 0 us
  Pallas kernels: 0 us -> 42.5 us
  starting transfers between devices: 34 us -> 0 us
  other arithmetic: 25.9 us -> 0 us
  waiting for transfers between devices: 18.2 us -> 0 us
  matrix products: 12.1 us -> 0 us
    scatter-add x8 -> x0, local copies, waits for them, and re-layouts: 53.6 us -> none  [the longest x7 53.5 us: gather_global(): summed = summed.at[:, :, along_x:along_x + count_x, along_y:along_y + cou...]
    psum x5 -> x0, blocking collectives: 43.6 us -> none  [over_axes(): return functools.reduce(lax.psum, axes, shard)]
    pallas_call x0 -> x1, Pallas kernels: none -> 42.5 us  [local(): pl.pallas_call(functools.partial(kernel, wide, narrow), out_shape=(jax.Sh...]
    ppermute x12 -> x0, starting transfers between devices: 34 us -> none  [the longest x4 15.7 us: with_halo(): before = lax.ppermute(last, axis, up)]
    ppermute x12 -> x0, waiting for transfers between devices: 18.2 us -> none  [the longest x4 9.53 us: with_halo(): after = lax.ppermute(initial, axis, down)]
    add x17 -> x0, other arithmetic: 14.8 us -> none  [the longest x6 5.98 us: gather_global(): summed = summed.at[:, :, along_x:along_x + count_x, along_y:along_y + cou...]
    dot_general x7 -> x0, matrix products: 12.1 us -> none  [the longest x1 4.87 us: element_contributions(): jnp.einsum('ij,bjxyz->bixyz', operator_matrix, stacked, precision=lax.Pre...]
    dot_general x3 -> x0, local copies, waits for them, and re-layouts: 5.39 us -> none  [aggregate(): jnp.dot(fine_stiff.reshape(-1, fine_stiff.shape[2]), coarse_averaging, pr...]
  transfers between devices with their start and end apart: 12 -> 0, of which waited for: 6 -> 0; matrix products, arithmetic and copies ran while one was open for 6% -> 0% of each run, Pallas kernels for 0% -> 0%
where the time goes in v1:
time: 47.6 us; the launch traced here: 47.5 us
  Pallas kernels  42.5 us (89%)
  local copies, waits for them, and re-layouts  4.35 us (9%)
  between operations  0.65 us (1%)
    pallas_call x1, Pallas kernels, local(): pl.pallas_call(functools.partial(kernel, wide, narrow), out_shape=(jax.Sh...  42.5 us
    unnamed x5, local copies, waits for them, and re-layouts  4.35 us

profile of v1, /device:TPU:1, one launch (start us, length us, event | category | flops | bytes accessed | tf_op | source)
XLA Modules:
  0.0 47.5 jit_solution(4020741937084863507)
XLA Ops:
  0.6 42.5 %shard_map.76 = (f32[9,4,16,128]{3,2,1,0:T(8,128)}, f32[3]{0:T(128)}, f32[12,48,384]{2,1,0:T(8,128)}) custom-call(f32[12,48,384]{2,1,0:T(8,128)} %design.1, s32[12,48,384]{2,1,0:T(8,128)} %passive.1, f32[9,4,16,128]{3,2,1,0:T(8,128)} %bitcast.3, s32[4,16,128]{2,1,0:T(8,128)} %support.1, s32[4,16,128]{2,1,0:T(8,128)} %loading.1), custom_call_target="tpu_custom_call" | custom-call | tf_op jit(solution)/shard_map/pallas_call | solution.py:631
  43.1 0.0 copy-start
  43.1 1.7 %copy.11 = f32[3,3,4,16,128]{4,3,2,1,0:T(8,128)} copy(f32[3,3,4,16,128]{4,3,2,1,0:T(8,128)} %bitcast.2) | data formatting | bytes 589824
  44.8 0.0 copy-done
  44.8 0.5 %copy.12 = f32[3]{0:T(128)} copy(f32[3]{0:T(128)S(1)} %copy-done) | data formatting | bytes 24
  45.4 2.1 %copy.13 = f32[12,48,384]{2,1,0:T(8,128)} copy(f32[12,48,384]{2,1,0:T(8,128)} %get-tuple-element.14) | data formatting | bytes 1769472
Async XLA Ops:
  43.1 1.7 %copy-start = (f32[3]{0:T(128)S(1)}, f32[3]{0:T(128)}, u32[]{:S(2)}) copy-start(f32[3]{0:T(128)} %get-tuple-element.13) | copy-start | bytes 40

commit v2 on v1

--- a/solution.py
+++ b/solution.py
@@ -107,13 +107,26 @@
     return sharpness / den * 3.0 * (1.0 - stiff_floor) / 27.0
 
 
+def banded(high, low, band, g):
+    h, l = (part[pl.ds(3 * g, 3)].reshape(144, DEEP) for part in (high, low))
+    b = band[...]
+    first, second = (
+        jnp.dot(h[:, k : k + 256], b, preferred_element_type=F32)
+        + jnp.dot(l[:, k : k + 256], b, preferred_element_type=F32)
+        for k in (0, 128)
+    )
+    lane = lax.broadcasted_iota(jnp.int32, (144, 128), 1)
+    middle = jnp.where(lane < 64, first[:, 128:256], second[:, 0:128])
+    return first[:, 0:128], middle, second[:, 128:256]
+
+
 def kernel(
     wide, narrow,
     design, passive, disp, support, loading,
-    res_out, comp_out, sens_out,
-    D, XF, AH, AL, PA, BL, T, EN, ESP, GX, OUT, V, M, FS, FXR, FYR, FDR, U, SU, LO, RES, MOD, S3,
-    WT, BAND, SPREAD, GATHER, AR1, AR2, RX,
-    lsem, osem, dss, drs, mss, mrs, bss, brs, ess, ers, fss, frs, a1s, a1r, a2s, a2r,
+    AH, AL, RES, COMP, BAND,
+    D, XF, PA, SW, BL, T, EN, ESP, GX, V, M, FS, FXR, FYR, FDR, U, SU, LO, MOD, S3,
+    WT, SPREAD, GATHER, AR1, AR2, RX,
+    lsem, dss, drs, mss, mrs, bss, brs, ess, ers, fss, frs, sss, srs, a1s, a1r, a2s, a2r,
 ):
     w = lax.axis_index("wide")
     n = lax.axis_index("narrow")
@@ -156,8 +169,8 @@
         pl.semaphore_signal(barrier, 1, device_id=peer2(k)[1], device_id_type=MESH)
 
     loads = [
-        pltpu.make_async_copy(disp, U, lsem.at[0]),
-        pltpu.make_async_copy(support, SU, lsem.at[1]),
+        pltpu.make_async_copy(disp, U.at[:, 0:4, 0:16, :], lsem.at[0]),
+        pltpu.make_async_copy(support, SU.at[0:4, 0:16, :], lsem.at[1]),
         pltpu.make_async_copy(design, D.at[3:15, 8:56, :], lsem.at[2]),
         pltpu.make_async_copy(loading, LO, lsem.at[3]),
     ] + [
@@ -166,61 +179,6 @@
     ]
     for copy in loads:
         copy.start()
-
-    def near(shape):
-        return lax.broadcasted_iota(jnp.int32, shape, 0), lax.broadcasted_iota(jnp.int32, shape, 1)
-
-    a, b = near((DEEP, DEEP))
-    BAND[...] = jnp.maximum(4 - jnp.abs(a - b), 0).astype(F32).astype(BF16)
-    a, b = near((EZ, DEEP))
-    gap = b - 3 * a
-    SPREAD[...] = jnp.where((gap >= 0) & (gap < 3), 1.0, 0.0).astype(BF16)
-    a, b = near((DEEP, EZ))
-    gap = a - 3 * b
-    GATHER[...] = jnp.where((gap >= 0) & (gap < 3), 1.0, 0.0).astype(BF16)
-    a, b = near((24, DEEP))
-    a = jnp.where(a == 23, -1, a)
-    deep = inverse_weight(b, DEEP)
-    for m in range(3):
-        WT[m] = inverse_weight(n * COLS + 3 * a + m, narrow * COLS) * deep
-    for x in range(18):
-        RX[x] = inverse_weight(w * ROWS + x - 3, wide * ROWS)
-
-    zero = functools.partial(jnp.zeros, dtype=F32)
-
-    @pl.when(w == 0)
-    def _():
-        D[0:3] = zero((3, 64, DEEP))
-        BL[0:3] = zero((3, 3, 32, DEEP))
-        EN[:, 0] = zero((3, 32, 128))
-        FXR[...] = zero((9, 16, 128))
-
-    @pl.when(w == wide - 1)
-    def _():
-        D[15:18] = zero((3, 64, DEEP))
-        BL[15:18] = zero((3, 3, 32, DEEP))
-        EN[:, 5] = zero((3, 32, 128))
-        M[:, 4] = zero((9, 24, 128))
-
-    @pl.when(n == 0)
-    def _():
-        D[:, 0:8] = zero((18, 8, DEEP))
-        BL[:, :, 0:8] = zero((18, 3, 8, DEEP))
-        EN[:, :, 0:8] = zero((3, 6, 8, 128))
-        FYR[...] = zero((9, 4, 8, 128))
-
-    @pl.when(n == narrow - 1)
-    def _():
-        D[:, 56:64] = zero((18, 8, DEEP))
-        BL[:, :, 24:32] = zero((18, 3, 8, DEEP))
-        EN[:, :, 24:32] = zero((3, 6, 8, 128))
-        M[:, :, 16:24] = zero((9, 5, 8, 128))
-
-    @pl.when((n == 0) | (w == 0))
-    def _():
-        FDR[...] = zero((9, 8, 128))
-
-    FS[...] = zero((9, 5, 24, 128))
 
     class Message:
         def __init__(self, src, dst, ss, rs, dw, dn):
@@ -264,33 +222,106 @@
         energies.append(
             Message(EN.at[:, sx, sy, :], EN.at[:, tx, ty, :], ess.at[d], ers.at[d], dw, dn)
         )
-    moves, forces = [], []
+    moves, holds, forces = [], [], []
     for d, (dw, dn) in enumerate(((-1, 0), (0, -1), (-1, -1))):
         sx, tx = x_part(dw, 0, 4, 1)
         sy, ty = x_part(dn, 0, 16, 1)
-        moves.append(Message(M.at[:, sx, sy, :], M.at[:, tx, ty, :], mss.at[d], mrs.at[d], dw, dn))
+        moves.append(
+            Message(disp.at[:, sx, sy, :], U.at[:, tx, ty, :], mss.at[d], mrs.at[d], dw, dn)
+        )
+        holds.append(
+            Message(support.at[sx, sy, :], SU.at[tx, ty, :], sss.at[d], srs.at[d], dw, dn)
+        )
     forces.append(Message(FS.at[:, 4, 0:16, :], FXR, fss.at[0], frs.at[0], 1, 0))
     forces.append(
         Message(FS.at[:, 0:4, 16:17, :], FYR.at[:, :, 0:1, :], fss.at[1], frs.at[1], 0, 1)
     )
     forces.append(Message(FS.at[:, 4, 16:17, :], FDR.at[:, 0:1, :], fss.at[2], frs.at[2], 1, 1))
 
+    pl.semaphore_wait(barrier, total)
+    for message in moves + holds + designs:
+        message.start()
+
+    def near(shape):
+        return lax.broadcasted_iota(jnp.int32, shape, 0), lax.broadcasted_iota(jnp.int32, shape, 1)
+
+    a, b = near((256, 256))
+    BAND[...] = jnp.maximum(4 - jnp.abs(a - b), 0).astype(F32).astype(BF16)
+    a, b = near((EZ, DEEP))
+    gap = b - 3 * a
+    SPREAD[...] = jnp.where((gap >= 0) & (gap < 3), 1.0, 0.0).astype(BF16)
+    a, b = near((DEEP, EZ))
+    gap = a - 3 * b
+    GATHER[...] = jnp.where((gap >= 0) & (gap < 3), 1.0, 0.0).astype(BF16)
+    a, b = near((24, DEEP))
+    a = jnp.where(a == 23, -1, a)
+    deep = inverse_weight(b, DEEP)
+    for m in range(3):
+        WT[m] = inverse_weight(n * COLS + 3 * a + m, narrow * COLS) * deep
+    for x in range(18):
+        RX[x] = inverse_weight(w * ROWS + x - 3, wide * ROWS)
+
+    zero = functools.partial(jnp.zeros, dtype=F32)
+
+    @pl.when(w == 0)
+    def _():
+        D[0:3] = zero((3, 64, DEEP))
+        BL[0:3] = zero((3, 3, 32, DEEP))
+        EN[:, 0] = zero((3, 32, 128))
+        FXR[...] = zero((9, 16, 128))
+
+    @pl.when(w == wide - 1)
+    def _():
+        D[15:18] = zero((3, 64, DEEP))
+        BL[15:18] = zero((3, 3, 32, DEEP))
+        EN[:, 5] = zero((3, 32, 128))
+        U[:, 4] = zero((9, 24, 128))
+
+    @pl.when(n == 0)
+    def _():
+        D[:, 0:8] = zero((18, 8, DEEP))
+        BL[:, :, 0:8] = zero((18, 3, 8, DEEP))
+        EN[:, :, 0:8] = zero((3, 6, 8, 128))
+        FYR[...] = zero((9, 4, 8, 128))
+
+    @pl.when(n == narrow - 1)
+    def _():
+        D[:, 56:64] = zero((18, 8, DEEP))
+        BL[:, :, 24:32] = zero((18, 3, 8, DEEP))
+        EN[:, :, 24:32] = zero((3, 6, 8, 128))
+        U[:, :, 16:24] = zero((9, 5, 8, 128))
+
+    @pl.when((n == 0) | (w == 0))
+    def _():
+        FDR[...] = zero((9, 8, 128))
+
+    FS[...] = zero((9, 5, 24, 128))
+
+    for copy in loads[4:]:
+        copy.wait()
+
+    def solid_step(x, _):
+        for m in range(3):
+            for t in range(2):
+                for c in range(3):
+                    void = PA[x, c, pl.ds(24 * t + m, 8, stride=3), :]
+                    rows, lanes = slice(8 * t, 8 * t + 8), slice(128 * c, 128 * c + 128)
+                    SW[x, m, rows, lanes] = (1.0 - void.astype(F32)) * (WT[m, rows, lanes] * RX[x + 3])
+        return 0
+
+    lax.fori_loop(0, ROWS, solid_step, 0)
+
     loads[0].wait()
     loads[1].wait()
-    free = 1.0 - SU[...].astype(F32)
-    for k in range(9):
-        M[k, 0:4, 0:16] = U[k] * free
-
-    pl.semaphore_wait(barrier, total)
-    for message in moves:
-        message.start()
-    for message in designs:
-        message.start()
+    for message in moves + holds:
+        message.wait_recv()
+    for l in range(5):
+        free = 1.0 - SU[l].astype(F32)
+        for k in range(9):
+            M[k, l] = U[k, l] * free
 
     modes = mode_matrix()
     lane = lax.broadcasted_iota(jnp.int32, (8, 128), 1)
-    for message in moves:
-        message.wait_recv()
 
     def energy_step(i, _):
         r, l = i // 4, i % 4
@@ -364,33 +395,20 @@
         return 0
 
     lax.fori_loop(0, ROWS, y_step, 0)
-    for copy in loads[4:]:
-        copy.wait()
-
-    def banded(g):
-        rows = pl.ds(3 * g, 3)
-        band = BAND[...]
-        return jnp.dot(
-            AH[rows].reshape(144, DEEP), band, preferred_element_type=F32
-        ) + jnp.dot(AL[rows].reshape(144, DEEP), band, preferred_element_type=F32)
 
     def z_step(g, _):
-        z = banded(g)
+        z = banded(AH, AL, BAND, g)
         for xr in range(3):
             x = 3 * g + xr
             for m in range(3):
-                value = z[16 * (3 * xr + m) : 16 * (3 * xr + m) + 16] * (WT[m, 0:16] * RX[x + 3])
-                for t in range(2):
-                    for c in range(3):
-                        void = PA[x, c, pl.ds(24 * t + m, 8, stride=3), :]
-                        part = value[8 * t : 8 * t + 8, 128 * c : 128 * c + 128]
-                        BL[x + 3, m, 8 + 8 * t : 16 + 8 * t, 128 * c : 128 * c + 128] = part * (
-                            1.0 - void.astype(F32)
-                        )
+                at = 16 * (3 * xr + m)
+                for c in range(3):
+                    lanes = slice(128 * c, 128 * c + 128)
+                    BL[x + 3, m, 8:24, lanes] = z[c][at : at + 16] * SW[x, m, :, lanes]
         return 0
 
     lax.fori_loop(0, 4, z_step, 0)
-    for message in fields:
+    for message in fields[2:]:
         message.start()
 
     def own_step(xe, _):
@@ -440,6 +458,8 @@
     phase2 = exchange(AR2, a2s, a2r, i2, count2, peer2)
     for send, _ in phase1:
         send.start()
+    for message in fields[:2]:
+        message.start()
 
     def force_step(i, _):
         r, l = i // 4, i % 4
@@ -489,10 +509,11 @@
     for message in energies:
         message.wait_recv()
     for r in range(3):
+        blocks = []
         for l in range(6):
-            edge = jnp.where(row8 == 7, EN[r, l, 0:8], EN[r, l, 24:32])
-            block = jnp.concatenate([EN[r, l, 8:24], edge], axis=0)
-            ESP[r, l] = times(block, SPREAD[...])
+            blocks.append(EN[r, l, 8:24])
+            blocks.append(jnp.where(row8 == 7, EN[r, l, 0:8], EN[r, l, 24:32]))
+        ESP[r] = times(jnp.concatenate(blocks, axis=0), SPREAD[...]).reshape(6, 24, DEEP)
 
     def own_terms(xe, _):
         for xr in range(3):
@@ -504,7 +525,7 @@
         return 0
 
     lax.fori_loop(0, 4, own_terms, 0)
-    for message in fields:
+    for message in fields[2:4]:
         message.wait_recv()
 
     def terms(x, xe, m, bl, rows):
@@ -513,15 +534,6 @@
             rho, slope = level(bl, thresholds[r])
             T[r, x, m, rows] = rho * rho * slope * (ESP[r, xe, rows] * scale)
 
-    for l in (0, 5):
-
-        def row_terms(xr, _, l=l):
-            for m in range(3):
-                terms(3 * l + xr, l, m, BL[3 * l + xr, m, 8:24, :], slice(0, 16))
-            return 0
-
-        lax.fori_loop(0, 3, row_terms, 0)
-
     def column_terms(x, _):
         for m in range(3):
             edge = lax.broadcasted_iota(jnp.int32, (8, DEEP), 0) == 7
@@ -529,7 +541,21 @@
             terms(x, x // 3, m, bl, slice(16, 24))
         return 0
 
-    lax.fori_loop(0, 18, column_terms, 0)
+    lax.fori_loop(3, 15, column_terms, 0)
+    for message in fields[4:]:
+        message.wait_recv()
+    for l in (0, 5):
+        lax.fori_loop(3 * l, 3 * l + 3, column_terms, 0)
+    for message in fields[:2]:
+        message.wait_recv()
+    for l in (0, 5):
+
+        def row_terms(xr, _, l=l):
+            for m in range(3):
+                terms(3 * l + xr, l, m, BL[3 * l + xr, m, 8:24, :], slice(0, 16))
+            return 0
+
+        lax.fori_loop(0, 3, row_terms, 0)
 
     for message in forces:
         message.wait_recv()
@@ -540,22 +566,20 @@
             lax.broadcasted_iota(jnp.int32, (4, 8, 128), 1) == 0, FYR[k], 0.0
         )
         FS[k, 0, 0:8] = FS[k, 0, 0:8] + jnp.where(row8 == 0, FDR[k], 0.0)
-    free = 1.0 - SU[...].astype(F32)
+    free = 1.0 - SU[0:4, 0:16].astype(F32)
     load = LO[...].astype(F32) * (-load_force)
     for k in range(9):
         stiff = FS[k, 0:4, 0:16]
         RES[k] = ((load - stiff) if k % 3 == 2 else (0.0 - stiff)) * free
-    res_copy = pltpu.make_async_copy(RES, res_out, osem.at[12])
-    res_copy.start()
 
     for _, recv in phase2:
         recv.wait_recv()
     total2 = AR2[0]
     for j in range(1, count2):
         total2 = total2 + AR2[j]
+    COMP[...] = total2
     scales = []
     for r in range(3):
-        comp_out[r] = jnp.sum(total2[r : r + 1])
         whole = jnp.sum(total2[r : r + 1], axis=1, keepdims=True)
         scales.append(jnp.broadcast_to(-slope_scale(thresholds[r]) / whole, (8, 128)))
 
@@ -590,6 +614,18 @@
 
     lax.fori_loop(0, ROWS, y_back, 0)
 
+    for message in moves + holds + designs + fields + energies + forces:
+        message.wait_send()
+    for send, _ in phase1 + phase2:
+        send.wait_send()
+
+
+def finish(AH, AL, RES, COMP, BAND, res_out, comp_out, sens_out, OUT, osem):
+    res_copy = pltpu.make_async_copy(RES, res_out, osem.at[12])
+    res_copy.start()
+    for r in range(3):
+        comp_out[r] = jnp.sum(COMP[r : r + 1])
+
     def out_copy(g, c):
         return pltpu.make_async_copy(
             OUT.at[pl.ds(3 * g, 3), c],
@@ -598,25 +634,18 @@
         )
 
     def z_back(g, _):
-        z = banded(g)
+        z = banded(AH, AL, BAND, g)
         for xr in range(3):
             for m in range(3):
                 for t in range(2):
                     for c in range(3):
                         at = 16 * (3 * xr + m) + 8 * t
-                        OUT[3 * g + xr, c, pl.ds(24 * t + m, 8, stride=3), :] = z[
-                            at : at + 8, 128 * c : 128 * c + 128
-                        ]
+                        OUT[3 * g + xr, c, pl.ds(24 * t + m, 8, stride=3), :] = z[c][at : at + 8]
         for c in range(3):
             out_copy(g, c).start()
         return 0
 
     lax.fori_loop(0, 4, z_back, 0)
-
-    for message in designs + moves + fields + energies + forces:
-        message.wait_send()
-    for send, _ in phase1 + phase2:
-        send.wait_send()
     res_copy.wait()
     for g in range(4):
         for c in range(3):
@@ -628,59 +657,71 @@
 
     def local(design, passive, displacement, support, loading):
         sems = pltpu.SemaphoreType.DMA
-        residual, compliance, sensitivity = pl.pallas_call(
+        vmem = pl.BlockSpec(memory_space=pltpu.VMEM)
+        hbm = pl.BlockSpec(memory_space=pltpu.MemorySpace.HBM)
+        passed = (
+            jax.ShapeDtypeStruct((ROWS, COLS, DEEP), BF16),
+            jax.ShapeDtypeStruct((ROWS, COLS, DEEP), BF16),
+            jax.ShapeDtypeStruct((9, EX, EY, EZ), F32),
+            jax.ShapeDtypeStruct((8, 128), F32),
+            jax.ShapeDtypeStruct((256, 256), BF16),
+        )
+        parts = pl.pallas_call(
             functools.partial(kernel, wide, narrow),
-            out_shape=(
-                jax.ShapeDtypeStruct((9, EX, EY, EZ), F32),
-                jax.ShapeDtypeStruct((3,), F32),
-                jax.ShapeDtypeStruct((ROWS, COLS, DEEP), F32),
-            ),
-            in_specs=[pl.BlockSpec(memory_space=pl.ANY)] * 5,
-            out_specs=(
-                pl.BlockSpec(memory_space=pl.ANY),
-                pl.BlockSpec(memory_space=pltpu.SMEM),
-                pl.BlockSpec(memory_space=pl.ANY),
-            ),
+            out_shape=passed,
+            in_specs=[hbm] * 5,
+            out_specs=(vmem,) * 5,
             scratch_shapes=[
                 pltpu.VMEM((18, 64, DEEP), F32),
                 pltpu.VMEM((ROWS, 3, 64, 128), F32),
-                pltpu.VMEM((ROWS, COLS, DEEP), BF16),
-                pltpu.VMEM((ROWS, COLS, DEEP), BF16),
                 pltpu.VMEM((ROWS, 3, COLS, 128), jnp.int32),
+                pltpu.VMEM((ROWS, 3, 16, DEEP), F32),
                 pltpu.VMEM((18, 3, 32, DEEP), F32),
                 pltpu.VMEM((3, 18, 3, 24, DEEP), F32),
                 pltpu.VMEM((3, 6, 32, 128), F32),
                 pltpu.VMEM((3, 6, 24, DEEP), F32),
                 pltpu.VMEM((ROWS, 3, 3, 32, 128), F32),
-                pltpu.VMEM((ROWS, 3, COLS, 128), F32),
                 pltpu.VMEM((12, 24, 16, 128), F32),
                 pltpu.VMEM((9, 5, 24, 128), F32),
                 pltpu.VMEM((9, 5, 24, 128), F32),
                 pltpu.VMEM((9, 16, 128), F32),
                 pltpu.VMEM((9, 4, 8, 128), F32),
                 pltpu.VMEM((9, 8, 128), F32),
-                pltpu.VMEM((9, EX, EY, EZ), F32),
+                pltpu.VMEM((9, 5, 24, 128), F32),
+                pltpu.VMEM((5, 24, 128), jnp.int32),
                 pltpu.VMEM((EX, EY, EZ), jnp.int32),
-                pltpu.VMEM((EX, EY, EZ), jnp.int32),
-                pltpu.VMEM((9, EX, EY, EZ), F32),
                 pltpu.VMEM((12, 16, 128), F32),
                 pltpu.VMEM((3, 4, 16, DEEP), F32),
                 pltpu.VMEM((3, 24, DEEP), F32),
-                pltpu.VMEM((DEEP, DEEP), BF16),
                 pltpu.VMEM((EZ, DEEP), BF16),
                 pltpu.VMEM((DEEP, EZ), BF16),
                 pltpu.VMEM((wide // 2, 8, 128), F32),
                 pltpu.VMEM((2 * narrow, 8, 128), F32),
                 pltpu.SMEM((18,), F32),
-                sems((7,)), sems((13,)),
+                sems((7,)),
                 sems((8,)), sems((8,)), sems((3,)), sems((3,)), sems((8,)), sems((8,)),
-                sems((8,)), sems((8,)), sems((3,)), sems((3,)),
+                sems((8,)), sems((8,)), sems((3,)), sems((3,)), sems((3,)), sems((3,)),
                 sems((wide // 2,)), sems((wide // 2,)), sems((2 * narrow,)), sems((2 * narrow,)),
             ],
             compiler_params=pltpu.CompilerParams(
-                collective_id=0, has_side_effects=True, vmem_limit_bytes=56 << 20
+                collective_id=0, has_side_effects=True, vmem_limit_bytes=40 << 20
             ),
-        )(design, passive, displacement.reshape(9, EX, EY, EZ), support, loading)
+        )(*(
+            pltpu.with_memory_space_constraint(a, pltpu.MemorySpace.HBM)
+            for a in (design, passive, displacement.reshape(9, EX, EY, EZ), support, loading)
+        ))
+        residual, compliance, sensitivity = pl.pallas_call(
+            finish,
+            out_shape=(
+                jax.ShapeDtypeStruct((9, EX, EY, EZ), F32),
+                jax.ShapeDtypeStruct((3,), F32),
+                jax.ShapeDtypeStruct((ROWS, COLS, DEEP), F32),
+            ),
+            in_specs=[vmem] * 5,
+            out_specs=(hbm, pl.BlockSpec(memory_space=pltpu.SMEM), hbm),
+            scratch_shapes=[pltpu.VMEM((ROWS, 3, COLS, 128), F32), sems((13,))],
+            compiler_params=pltpu.CompilerParams(vmem_limit_bytes=8 << 20),
+        )(*parts)
         return residual.reshape(3, 3, EX, EY, EZ), compliance, sensitivity
 
     in_specs = (

time: 47.6 us -> 43.2 us (0.908)
  local copies, waits for them, and re-layouts: 4.35 us -> 0 us
    unnamed x5 -> x0, local copies, waits for them, and re-layouts: 4.35 us -> none
    pallas_call x1 -> x2, Pallas kernels: 42.5 us -> 42.5 us  [the longest x1 40 us: local(): pl.pallas_call(functools.partial(kernel, wide, narrow), out_shape=passed,...]
where the time goes in v2:
time: 43.2 us; the launch traced here: 43.1 us
  Pallas kernels  42.5 us (98%)
  between operations  0.64 us (1%)
    pallas_call x1, Pallas kernels, local(): pl.pallas_call(functools.partial(kernel, wide, narrow), out_shape=passed,...  40 us
    pallas_call x1, Pallas kernels, local(): pl.pallas_call(finish, out_shape=(jax.ShapeDtypeStruct((9, EX, EY, EZ), F...  2.41 us

profile of v2, /device:TPU:1, one launch (start us, length us, event | category | flops | bytes accessed | tf_op | source)
XLA Modules:
  0.0 43.1 jit_solution(12142137095455901108)
XLA Ops:
  0.6 40.0 %shard_map.76 = (bf16[12,48,384]{2,1,0:T(8,128)(2,1)S(1)}, bf16[12,48,384]{2,1,0:T(8,128)(2,1)S(1)}, f32[9,4,16,128]{3,2,1,0:T(8,128)S(1)}, f32[8,128]{1,0:T(8,128)S(1)}, bf16[256,256]{1,0:T(8,128)(2,1)S(1)}) custom-call(f32[12,48,384]{2,1,0:T(8,128)} %design.1, s32[12,48,384]{2,1,0:T(8,128)} %passive.1, f32[9,4,16,128]{3,2,1,0:T(8,128)} %bitcast.2, ...), custom_call_target="tpu_custom_call" | custom-call | tf_op jit(solution)/shard_map/pallas_call | solution.py:669
  40.7 2.4 %shard_map.77 = (f32[9,4,16,128]{3,2,1,0:T(8,128)}, f32[3]{0:T(128)}, f32[12,48,384]{2,1,0:T(8,128)}) custom-call(bf16[12,48,384]{2,1,0:T(8,128)(2,1)S(1)} %get-tuple-element.11.AH, bf16[12,48,384]{2,1,0:T(8,128)(2,1)S(1)} %get-tuple-element.12.AL, f32[9,4,16,128]{3,2,1,0:T(8,128)S(1)} %get-tuple-element.13.RES, f32[8,128]{1,0:T(8,128)S(1)} %get-tuple-element.14.COMP, ...), custom_call_target="tpu_custom_call" | custom-call | tf_op jit(solution)/shard_map/pallas_call | solution.py:713

commit v3 on v2

--- a/solution.py
+++ b/solution.py
@@ -96,35 +96,49 @@
 
 def level(bl, eta):
     low = math.tanh(sharpness * eta)
-    den = low + math.tanh(sharpness * (1.0 - eta))
     t = jnp.tanh(bl * sharpness - sharpness * eta)
-    rho = t * (1.0 / den) + low / den
-    return rho, 1.0 - t * t
+    return t + low, 1.0 - t * t
+
+
+def denominator(eta):
+    return math.tanh(sharpness * eta) + math.tanh(sharpness * (1.0 - eta))
 
 
 def slope_scale(eta):
-    den = math.tanh(sharpness * eta) + math.tanh(sharpness * (1.0 - eta))
-    return sharpness / den * 3.0 * (1.0 - stiff_floor) / 27.0
-
-
-def banded(high, low, band, g):
-    h, l = (part[pl.ds(3 * g, 3)].reshape(144, DEEP) for part in (high, low))
+    return sharpness / denominator(eta) ** 3 * 3.0 * (1.0 - stiff_floor) / 27.0
+
+
+def banded(high, low, band, groups):
+    h, l = (
+        jnp.concatenate([part[3 * g : 3 * g + 3].reshape(144, DEEP) for g in groups], axis=0)
+        for part in (high, low)
+    )
     b = band[...]
     first, second = (
         jnp.dot(h[:, k : k + 256], b, preferred_element_type=F32)
         + jnp.dot(l[:, k : k + 256], b, preferred_element_type=F32)
         for k in (0, 128)
     )
-    lane = lax.broadcasted_iota(jnp.int32, (144, 128), 1)
+    lane = lax.broadcasted_iota(jnp.int32, (144 * len(groups), 128), 1)
     middle = jnp.where(lane < 64, first[:, 128:256], second[:, 0:128])
     return first[:, 0:128], middle, second[:, 128:256]
+
+
+def keep(AH, AL, x, parts):
+    for m in range(3):
+        block = jnp.concatenate(
+            [jnp.concatenate([parts[m, t, c] for t in range(2)], axis=0) for c in range(3)], axis=1
+        )
+        high, low = split(block)
+        AH[x, 16 * m : 16 * m + 16, :] = high
+        AL[x, 16 * m : 16 * m + 16, :] = low
 
 
 def kernel(
     wide, narrow,
     design, passive, disp, support, loading,
-    AH, AL, RES, COMP, BAND,
-    D, XF, PA, SW, BL, T, EN, ESP, GX, V, M, FS, FXR, FYR, FDR, U, SU, LO, MOD, S3,
+    GX, RES, COMP, BAND,
+    AH, AL, D, XF, PA, SW, BL, T, EN, ESP, V, M, FS, FXR, FYR, FDR, U, SU, LO, MOD, S3,
     WT, SPREAD, GATHER, AR1, AR2, RX,
     lsem, dss, drs, mss, mrs, bss, brs, ess, ers, fss, frs, sss, srs, a1s, a1r, a2s, a2r,
 ):
@@ -145,11 +159,11 @@
 
     def peer1(k):
         j = (i1 + k) % count1
-        return j, ((j // 2) * 4 + xl * 2 + j % 2, n)
+        return (j // 2) * 4 + xl * 2 + j % 2, n
 
     def peer2(k):
         j = (i2 + k) % count2
-        return j, (zc * 4 + (j // narrow) * 2 + core, j % narrow)
+        return zc * 4 + (j // narrow) * 2 + core, j % narrow
 
     def around(dw, dn):
         return ((w + dw + wide) % wide, (n + dn + narrow) % narrow)
@@ -164,9 +178,9 @@
             pl.semaphore_signal(barrier, 1, device_id=around(dw, dn), device_id_type=MESH)
 
     for k in range(1, count1):
-        pl.semaphore_signal(barrier, 1, device_id=peer1(k)[1], device_id_type=MESH)
+        pl.semaphore_signal(barrier, 1, device_id=peer1(k), device_id_type=MESH)
     for k in range(1, count2):
-        pl.semaphore_signal(barrier, 1, device_id=peer2(k)[1], device_id_type=MESH)
+        pl.semaphore_signal(barrier, 1, device_id=peer2(k), device_id_type=MESH)
 
     loads = [
         pltpu.make_async_copy(disp, U.at[:, 0:4, 0:16, :], lsem.at[0]),
@@ -239,7 +253,7 @@
     forces.append(Message(FS.at[:, 4, 16:17, :], FDR.at[:, 0:1, :], fss.at[2], frs.at[2], 1, 1))
 
     pl.semaphore_wait(barrier, total)
-    for message in moves + holds + designs:
+    for message in moves[1:] + holds[1:] + designs + moves[:1] + holds[:1]:
         message.start()
 
     def near(shape):
@@ -313,18 +327,22 @@
 
     loads[0].wait()
     loads[1].wait()
-    for message in moves + holds:
-        message.wait_recv()
-    for l in range(5):
+
+    def moved(l):
         free = 1.0 - SU[l].astype(F32)
         for k in range(9):
             M[k, l] = U[k, l] * free
 
+    for message in (moves[1], holds[1]):
+        message.wait_recv()
+    for l in range(4):
+        moved(l)
+
     modes = mode_matrix()
     lane = lax.broadcasted_iota(jnp.int32, (8, 128), 1)
 
-    def energy_step(i, _):
-        r, l = i // 4, i % 4
+    def energy_step(r, l):
+        i = r * 4 + l
         for t in range(2):
             hat = [None] * 24
             for comp in range(3):
@@ -355,11 +373,16 @@
                 term = value * hat[row]
                 energy = term if energy is None else energy + term
             EN[r, 1 + l, 8 + 8 * t : 16 + 8 * t] = energy
-        return 0
-
-    lax.fori_loop(0, 12, energy_step, 0)
-    for message in energies:
-        message.start()
+
+    def inner_energies(j, _):
+        energy_step(j // 3, j % 3)
+        return 0
+
+    def last_energies(r, _):
+        energy_step(r, 3)
+        return 0
+
+    lax.fori_loop(0, 9, inner_energies, 0)
 
     loads[2].wait()
     for message in designs:
@@ -374,15 +397,6 @@
         return 0
 
     lax.fori_loop(0, 8, x_step, 0)
-
-    def keep(x, parts):
-        for m in range(3):
-            block = jnp.concatenate(
-                [jnp.concatenate([parts[m, t, c] for t in range(2)], axis=0) for c in range(3)], axis=1
-            )
-            high, low = split(block)
-            AH[x, 16 * m : 16 * m + 16, :] = high
-            AL[x, 16 * m : 16 * m + 16, :] = low
 
     def y_step(x, _):
         parts = {}
@@ -391,23 +405,32 @@
                 out = tent([XF[x, c, pl.ds(8 + 24 * t + k, 8, stride=3), :] for k in range(-3, 6)])
                 for m in range(3):
                     parts[m, t, c] = out[m]
-        keep(x, parts)
+        keep(AH, AL, x, parts)
         return 0
 
     lax.fori_loop(0, ROWS, y_step, 0)
 
-    def z_step(g, _):
-        z = banded(AH, AL, BAND, g)
-        for xr in range(3):
-            x = 3 * g + xr
-            for m in range(3):
-                at = 16 * (3 * xr + m)
-                for c in range(3):
-                    lanes = slice(128 * c, 128 * c + 128)
-                    BL[x + 3, m, 8:24, lanes] = z[c][at : at + 16] * SW[x, m, :, lanes]
-        return 0
-
-    lax.fori_loop(0, 4, z_step, 0)
+    def z_step(groups):
+        z = banded(AH, AL, BAND, groups)
+        for i, g in enumerate(groups):
+            for xr in range(3):
+                x = 3 * g + xr
+                for m in range(3):
+                    at = 144 * i + 16 * (3 * xr + m)
+                    for c in range(3):
+                        lanes = slice(128 * c, 128 * c + 128)
+                        BL[x + 3, m, 8:24, lanes] = z[c][at : at + 16] * SW[x, m, :, lanes]
+
+    z_step((0, 3))
+    for message in fields[:2]:
+        message.start()
+    for message in (moves[0], holds[0], moves[2], holds[2]):
+        message.wait_recv()
+    moved(4)
+    lax.fori_loop(0, 3, last_energies, 0)
+    for message in energies:
+        message.start()
+    z_step((1, 2))
     for message in fields[2:]:
         message.start()
 
@@ -417,18 +440,18 @@
             for m in range(3):
                 bl = BL[3 + 3 * xe + xr, m, 8:24, :]
                 for r in range(3):
-                    rho, slope = level(bl, thresholds[r])
-                    square = rho * rho
-                    T[r, 3 + 3 * xe + xr, m, 0:16] = square * slope
-                    cube = square * rho
+                    rho, _ = level(bl, thresholds[r])
+                    cube = rho * rho * rho
                     sums[r] = cube if sums[r] is None else sums[r] + cube
         for r in range(3):
             S3[r, xe] = sums[r]
         return 0
 
     lax.fori_loop(0, 4, own_step, 0)
-    moduli = times(S3[...].reshape(192, DEEP), GATHER[...]) * ((1.0 - stiff_floor) / 27.0) + stiff_floor
-    MOD[...] = moduli.reshape(12, 16, 128)
+    moduli = times(S3[...].reshape(192, DEEP), GATHER[...]).reshape(12, 16, 128)
+    for r in range(3):
+        scale = (1.0 - stiff_floor) / 27.0 / denominator(thresholds[r]) ** 3
+        MOD[4 * r : 4 * r + 4] = moduli[4 * r : 4 * r + 4] * scale + stiff_floor
     row8 = lax.broadcasted_iota(jnp.int32, (8, 128), 0)
     tile = zero((8, 128))
     for r in range(3):
@@ -440,26 +463,18 @@
     AR1[i1] = tile
 
     def exchange(buf, ss, rs, me, count, peer):
-        out = []
-        for k in range(1, count):
-            j, device = peer(k)
-            send = pltpu.make_async_remote_copy(
-                src_ref=buf.at[me], dst_ref=buf.at[me], send_sem=ss.at[k], recv_sem=rs.at[me],
-                device_id=device, device_id_type=MESH,
+        def remote(part, device):
+            return pltpu.make_async_remote_copy(
+                src_ref=part, dst_ref=part, send_sem=ss, recv_sem=rs, device_id=device, device_id_type=MESH
             )
-            recv = pltpu.make_async_remote_copy(
-                src_ref=buf.at[j], dst_ref=buf.at[j], send_sem=ss.at[k], recv_sem=rs.at[j],
-                device_id=device, device_id_type=MESH,
-            )
-            out.append((send, recv))
-        return out
-
-    phase1 = exchange(AR1, a1s, a1r, i1, count1, peer1)
-    phase2 = exchange(AR2, a2s, a2r, i2, count2, peer2)
-    for send, _ in phase1:
+
+        whole = remote(buf.at[pl.ds(0, count - 1)], peer(1))
+        return [remote(buf.at[me], peer(k)) for k in range(1, count)], whole
+
+    sends1, whole1 = exchange(AR1, a1s, a1r, i1, count1, peer1)
+    sends2, whole2 = exchange(AR2, a2s, a2r, i2, count2, peer2)
+    for send in sends1:
         send.start()
-    for message in fields[:2]:
-        message.start()
 
     def force_step(i, _):
         r, l = i // 4, i % 4
@@ -494,39 +509,9 @@
         return 0
 
     lax.fori_loop(0, 12, force_step, 0)
-    for message in forces:
-        message.start()
-
-    for _, recv in phase1:
-        recv.wait_recv()
-    total1 = AR1[0]
-    for j in range(1, count1):
-        total1 = total1 + AR1[j]
-    AR2[i2] = total1
-    for send, _ in phase2:
-        send.start()
-
-    for message in energies:
-        message.wait_recv()
-    for r in range(3):
-        blocks = []
-        for l in range(6):
-            blocks.append(EN[r, l, 8:24])
-            blocks.append(jnp.where(row8 == 7, EN[r, l, 0:8], EN[r, l, 24:32]))
-        ESP[r] = times(jnp.concatenate(blocks, axis=0), SPREAD[...]).reshape(6, 24, DEEP)
-
-    def own_terms(xe, _):
-        for xr in range(3):
-            x = 3 + 3 * xe + xr
-            for m in range(3):
-                scale = WT[m, 0:16] * RX[x]
-                for r in range(3):
-                    T[r, x, m, 0:16] = T[r, x, m, 0:16] * (ESP[r, 1 + xe, 0:16] * scale)
-        return 0
-
-    lax.fori_loop(0, 4, own_terms, 0)
-    for message in fields[2:4]:
-        message.wait_recv()
+
+    block = jnp.concatenate([EN[r, l, 8:24] for r in range(3) for l in range(1, 5)], axis=0)
+    ESP[:, 1:5, 0:16] = times(block, SPREAD[...]).reshape(3, 4, 16, DEEP)
 
     def terms(x, xe, m, bl, rows):
         scale = WT[m, rows] * RX[x]
@@ -534,6 +519,11 @@
             rho, slope = level(bl, thresholds[r])
             T[r, x, m, rows] = rho * rho * slope * (ESP[r, xe, rows] * scale)
 
+    def row_terms(x, _):
+        for m in range(3):
+            terms(x, x // 3, m, BL[x, m, 8:24, :], slice(0, 16))
+        return 0
+
     def column_terms(x, _):
         for m in range(3):
             edge = lax.broadcasted_iota(jnp.int32, (8, DEEP), 0) == 7
@@ -541,21 +531,42 @@
             terms(x, x // 3, m, bl, slice(16, 24))
         return 0
 
+    lax.fori_loop(3, 15, row_terms, 0)
+
+    whole1.wait_recv()
+    total1 = AR1[0]
+    for j in range(1, count1):
+        total1 = total1 + AR1[j]
+    AR2[i2] = total1
+    for send in sends2:
+        send.start()
+    for message in forces:
+        message.start()
+
+    for message in energies:
+        message.wait_recv()
+    blocks = []
+    for r in range(3):
+        blocks += [EN[r, 0, 8:24], EN[r, 5, 8:24]]
+        for l in range(6):
+            blocks.append(jnp.where(row8 == 7, EN[r, l, 0:8], EN[r, l, 24:32]))
+    block = times(jnp.concatenate(blocks, axis=0), SPREAD[...])
+    for r in range(3):
+        ESP[r, 0, 0:16] = block[80 * r : 80 * r + 16]
+        ESP[r, 5, 0:16] = block[80 * r + 16 : 80 * r + 32]
+        for l in range(6):
+            ESP[r, l, 16:24] = block[80 * r + 32 + 8 * l : 80 * r + 40 + 8 * l]
+    for message in fields[:2]:
+        message.wait_recv()
+    for l in (0, 15):
+        lax.fori_loop(l, l + 3, row_terms, 0)
+    for message in fields[2:4]:
+        message.wait_recv()
     lax.fori_loop(3, 15, column_terms, 0)
     for message in fields[4:]:
         message.wait_recv()
-    for l in (0, 5):
-        lax.fori_loop(3 * l, 3 * l + 3, column_terms, 0)
-    for message in fields[:2]:
-        message.wait_recv()
-    for l in (0, 5):
-
-        def row_terms(xr, _, l=l):
-            for m in range(3):
-                terms(3 * l + xr, l, m, BL[3 * l + xr, m, 8:24, :], slice(0, 16))
-            return 0
-
-        lax.fori_loop(0, 3, row_terms, 0)
+    for l in (0, 15):
+        lax.fori_loop(l, l + 3, column_terms, 0)
 
     for message in forces:
         message.wait_recv()
@@ -572,8 +583,7 @@
         stiff = FS[k, 0:4, 0:16]
         RES[k] = ((load - stiff) if k % 3 == 2 else (0.0 - stiff)) * free
 
-    for _, recv in phase2:
-        recv.wait_recv()
+    whole2.wait_recv()
     total2 = AR2[0]
     for j in range(1, count2):
         total2 = total2 + AR2[j]
@@ -602,6 +612,25 @@
 
     lax.fori_loop(0, 3, x_back, 0)
 
+    for message in moves + holds + designs + fields + energies + forces:
+        message.wait_send()
+    whole1.wait_send()
+    whole2.wait_send()
+
+
+def finish(GX, RES, COMP, BAND, res_out, comp_out, sens_out, AH, AL, OUT, osem):
+    res_copy = pltpu.make_async_copy(RES, res_out, osem.at[6])
+    res_copy.start()
+    for r in range(3):
+        comp_out[r] = jnp.sum(COMP[r : r + 1])
+
+    def out_copy(g, c):
+        return pltpu.make_async_copy(
+            OUT.at[pl.ds(6 * g, 6), c],
+            sens_out.at[pl.ds(6 * g, 6), :, 128 * c : 128 * c + 128],
+            osem.at[3 * g + c],
+        )
+
     def y_back(x, _):
         parts = {}
         for t in range(2):
@@ -609,45 +638,21 @@
                 out = tent([GX[x, k % 3, c, pl.ds(8 + 8 * t + k // 3, 8), :] for k in range(-3, 6)])
                 for m in range(3):
                     parts[m, t, c] = out[m]
-        keep(x, parts)
-        return 0
-
-    lax.fori_loop(0, ROWS, y_back, 0)
-
-    for message in moves + holds + designs + fields + energies + forces:
-        message.wait_send()
-    for send, _ in phase1 + phase2:
-        send.wait_send()
-
-
-def finish(AH, AL, RES, COMP, BAND, res_out, comp_out, sens_out, OUT, osem):
-    res_copy = pltpu.make_async_copy(RES, res_out, osem.at[12])
-    res_copy.start()
-    for r in range(3):
-        comp_out[r] = jnp.sum(COMP[r : r + 1])
-
-    def out_copy(g, c):
-        return pltpu.make_async_copy(
-            OUT.at[pl.ds(3 * g, 3), c],
-            sens_out.at[pl.ds(3 * g, 3), :, 128 * c : 128 * c + 128],
-            osem.at[3 * g + c],
-        )
-
-    def z_back(g, _):
-        z = banded(AH, AL, BAND, g)
-        for xr in range(3):
-            for m in range(3):
-                for t in range(2):
-                    for c in range(3):
+        keep(AH, AL, x, parts)
+        return 0
+
+    for g in range(2):
+        lax.fori_loop(6 * g, 6 * g + 6, y_back, 0)
+        z = banded(AH, AL, BAND, (2 * g, 2 * g + 1))
+        for c in range(3):
+            for xr in range(6):
+                for m in range(3):
+                    for t in range(2):
                         at = 16 * (3 * xr + m) + 8 * t
-                        OUT[3 * g + xr, c, pl.ds(24 * t + m, 8, stride=3), :] = z[c][at : at + 8]
-        for c in range(3):
+                        OUT[6 * g + xr, c, pl.ds(24 * t + m, 8, stride=3), :] = z[c][at : at + 8]
             out_copy(g, c).start()
-        return 0
-
-    lax.fori_loop(0, 4, z_back, 0)
     res_copy.wait()
-    for g in range(4):
+    for g in range(2):
         for c in range(3):
             out_copy(g, c).wait()
 
@@ -660,8 +665,7 @@
         vmem = pl.BlockSpec(memory_space=pltpu.VMEM)
         hbm = pl.BlockSpec(memory_space=pltpu.MemorySpace.HBM)
         passed = (
-            jax.ShapeDtypeStruct((ROWS, COLS, DEEP), BF16),
-            jax.ShapeDtypeStruct((ROWS, COLS, DEEP), BF16),
+            jax.ShapeDtypeStruct((ROWS, 3, 3, 32, 128), F32),
             jax.ShapeDtypeStruct((9, EX, EY, EZ), F32),
             jax.ShapeDtypeStruct((8, 128), F32),
             jax.ShapeDtypeStruct((256, 256), BF16),
@@ -670,8 +674,10 @@
             functools.partial(kernel, wide, narrow),
             out_shape=passed,
             in_specs=[hbm] * 5,
-            out_specs=(vmem,) * 5,
+            out_specs=(vmem,) * 4,
             scratch_shapes=[
+                pltpu.VMEM((ROWS, COLS, DEEP), BF16),
+                pltpu.VMEM((ROWS, COLS, DEEP), BF16),
                 pltpu.VMEM((18, 64, DEEP), F32),
                 pltpu.VMEM((ROWS, 3, 64, 128), F32),
                 pltpu.VMEM((ROWS, 3, COLS, 128), jnp.int32),
@@ -680,7 +686,6 @@
                 pltpu.VMEM((3, 18, 3, 24, DEEP), F32),
                 pltpu.VMEM((3, 6, 32, 128), F32),
                 pltpu.VMEM((3, 6, 24, DEEP), F32),
-                pltpu.VMEM((ROWS, 3, 3, 32, 128), F32),
                 pltpu.VMEM((12, 24, 16, 128), F32),
                 pltpu.VMEM((9, 5, 24, 128), F32),
                 pltpu.VMEM((9, 5, 24, 128), F32),
@@ -701,7 +706,7 @@
                 sems((7,)),
                 sems((8,)), sems((8,)), sems((3,)), sems((3,)), sems((8,)), sems((8,)),
                 sems((8,)), sems((8,)), sems((3,)), sems((3,)), sems((3,)), sems((3,)),
-                sems((wide // 2,)), sems((wide // 2,)), sems((2 * narrow,)), sems((2 * narrow,)),
+                sems, sems, sems, sems,
             ],
             compiler_params=pltpu.CompilerParams(
                 collective_id=0, has_side_effects=True, vmem_limit_bytes=40 << 20
@@ -717,9 +722,14 @@
                 jax.ShapeDtypeStruct((3,), F32),
                 jax.ShapeDtypeStruct((ROWS, COLS, DEEP), F32),
             ),
-            in_specs=[vmem] * 5,
+            in_specs=[vmem] * 4,
             out_specs=(hbm, pl.BlockSpec(memory_space=pltpu.SMEM), hbm),
-            scratch_shapes=[pltpu.VMEM((ROWS, 3, COLS, 128), F32), sems((13,))],
+            scratch_shapes=[
+                pltpu.VMEM((ROWS, COLS, DEEP), BF16),
+                pltpu.VMEM((ROWS, COLS, DEEP), BF16),
+                pltpu.VMEM((ROWS, 3, COLS, 128), F32),
+                sems((7,)),
+            ],
             compiler_params=pltpu.CompilerParams(vmem_limit_bytes=8 << 20),
         )(*parts)
         return residual.reshape(3, 3, EX, EY, EZ), compliance, sensitivity

time: 43.2 us -> 40.9 us (0.947)
  Pallas kernels: 42.5 us -> 40.2 us
    pallas_call x1, Pallas kernels: 40 us -> 37.7 us  [local(): pl.pallas_call(functools.partial(kernel, wide, narrow), out_shape=passed,...]
where the time goes in v3:
time: 40.9 us; the launch traced here: 40.8 us
  Pallas kernels  40.2 us (98%)
  between operations  0.64 us (2%)
    pallas_call x1, Pallas kernels, local(): pl.pallas_call(functools.partial(kernel, wide, narrow), out_shape=passed,...  37.7 us
    pallas_call x1, Pallas kernels, local(): pl.pallas_call(finish, out_shape=(jax.ShapeDtypeStruct((9, EX, EY, EZ), F...  2.54 us

profile of v3, /device:TPU:1, one launch (start us, length us, event | category | flops | bytes accessed | tf_op | source)
XLA Modules:
  0.0 40.8 jit_solution(7077751861243402517)
XLA Ops:
  0.6 37.7 %shard_map.76 = (f32[12,3,3,32,128]{4,3,2,1,0:T(8,128)S(1)}, f32[9,4,16,128]{3,2,1,0:T(8,128)S(1)}, f32[8,128]{1,0:T(8,128)S(1)}, bf16[256,256]{1,0:T(8,128)(2,1)S(1)}) custom-call(f32[12,48,384]{2,1,0:T(8,128)} %design.1, s32[12,48,384]{2,1,0:T(8,128)} %passive.1, f32[9,4,16,128]{3,2,1,0:T(8,128)} %bitcast.2, s32[4,16,128]{2,1,0:T(8,128)} %support.1, ...), custom_call_target="tpu_custom_call" | custom-call | tf_op jit(solution)/shard_map/pallas_call | solution.py:673
  38.3 2.5 %shard_map.77 = (f32[9,4,16,128]{3,2,1,0:T(8,128)}, f32[3]{0:T(128)}, f32[12,48,384]{2,1,0:T(8,128)}) custom-call(f32[12,3,3,32,128]{4,3,2,1,0:T(8,128)S(1)} %get-tuple-element.10.GX, f32[9,4,16,128]{3,2,1,0:T(8,128)S(1)} %get-tuple-element.11.RES, f32[8,128]{1,0:T(8,128)S(1)} %get-tuple-element.12.COMP, bf16[256,256]{1,0:T(8,128)(2,1)S(1)} %get-tuple-element.13.BAND), custom_call_target="tpu_custom_call" | custom-call | tf_op jit(solution)/shard_map/pallas_call | solution.py:718

commit v4 on v3

--- a/solution.py
+++ b/solution.py
@@ -253,7 +253,7 @@
     forces.append(Message(FS.at[:, 4, 16:17, :], FDR.at[:, 0:1, :], fss.at[2], frs.at[2], 1, 1))
 
     pl.semaphore_wait(barrier, total)
-    for message in moves[1:] + holds[1:] + designs + moves[:1] + holds[:1]:
+    for message in moves[1:] + holds[1:] + designs[2:] + designs[:2] + moves[:1] + holds[:1]:
         message.start()
 
     def near(shape):
@@ -383,6 +383,10 @@
         return 0
 
     lax.fori_loop(0, 9, inner_energies, 0)
+    early = [message for message, d in zip(energies, DIRS) if d[0] < 0]
+    late = [message for message, d in zip(energies, DIRS) if d[0] >= 0]
+    for message in early:
+        message.start()
 
     loads[2].wait()
     for message in designs:
@@ -422,17 +426,17 @@
                         BL[x + 3, m, 8:24, lanes] = z[c][at : at + 16] * SW[x, m, :, lanes]
 
     z_step((0, 3))
-    for message in fields[:2]:
+    z_step((1, 2))
+    for message in fields[2:]:
         message.start()
+    fields[1].start()
     for message in (moves[0], holds[0], moves[2], holds[2]):
         message.wait_recv()
     moved(4)
     lax.fori_loop(0, 3, last_energies, 0)
-    for message in energies:
+    for message in late:
         message.start()
-    z_step((1, 2))
-    for message in fields[2:]:
-        message.start()
+    fields[0].start()
 
     def own_step(xe, _):
         sums = [None] * 3
@@ -453,14 +457,16 @@
         scale = (1.0 - stiff_floor) / 27.0 / denominator(thresholds[r]) ** 3
         MOD[4 * r : 4 * r + 4] = moduli[4 * r : 4 * r + 4] * scale + stiff_floor
     row8 = lax.broadcasted_iota(jnp.int32, (8, 128), 0)
-    tile = zero((8, 128))
+    spot = lax.broadcasted_iota(jnp.int32, (1, 128), 1)
+    line = zero((1, 128))
     for r in range(3):
         part = zero((8, 128))
         for l in range(4):
             for t in range(2):
                 part = part + MOD[4 * r + l, 8 * t : 8 * t + 8] * EN[r, 1 + l, 8 + 8 * t : 16 + 8 * t]
-        tile = jnp.where(row8 == r, jnp.sum(part, axis=0, keepdims=True), tile)
-    AR1[i1] = tile
+        part = jnp.sum(jnp.sum(part, axis=0, keepdims=True), axis=1, keepdims=True)
+        line = jnp.where(spot == r, part, line)
+    AR1[pl.ds(i1, 1), :] = line
 
     def exchange(buf, ss, rs, me, count, peer):
         def remote(part, device):
@@ -469,7 +475,7 @@
             )
 
         whole = remote(buf.at[pl.ds(0, count - 1)], peer(1))
-        return [remote(buf.at[me], peer(k)) for k in range(1, count)], whole
+        return [remote(buf.at[pl.ds(me, 1)], peer(k)) for k in range(1, count)], whole
 
     sends1, whole1 = exchange(AR1, a1s, a1r, i1, count1, peer1)
     sends2, whole2 = exchange(AR2, a2s, a2r, i2, count2, peer2)
@@ -534,10 +540,7 @@
     lax.fori_loop(3, 15, row_terms, 0)
 
     whole1.wait_recv()
-    total1 = AR1[0]
-    for j in range(1, count1):
-        total1 = total1 + AR1[j]
-    AR2[i2] = total1
+    AR2[pl.ds(i2, 1), :] = jnp.sum(AR1[...], axis=0, keepdims=True)
     for send in sends2:
         send.start()
     for message in forces:
@@ -584,14 +587,11 @@
         RES[k] = ((load - stiff) if k % 3 == 2 else (0.0 - stiff)) * free
 
     whole2.wait_recv()
-    total2 = AR2[0]
-    for j in range(1, count2):
-        total2 = total2 + AR2[j]
-    COMP[...] = total2
-    scales = []
-    for r in range(3):
-        whole = jnp.sum(total2[r : r + 1], axis=1, keepdims=True)
-        scales.append(jnp.broadcast_to(-slope_scale(thresholds[r]) / whole, (8, 128)))
+    whole = jnp.sum(AR2[...], axis=0, keepdims=True)
+    COMP[...] = jnp.broadcast_to(whole, (8, 128))
+    scales = [
+        jnp.broadcast_to(-slope_scale(thresholds[r]) / whole[:, r : r + 1], (8, 128)) for r in range(3)
+    ]
 
     def x_back(m, _):
         for t in range(3):
@@ -621,8 +621,9 @@
 def finish(GX, RES, COMP, BAND, res_out, comp_out, sens_out, AH, AL, OUT, osem):
     res_copy = pltpu.make_async_copy(RES, res_out, osem.at[6])
     res_copy.start()
+    spot = lax.broadcasted_iota(jnp.int32, (1, 128), 1)
     for r in range(3):
-        comp_out[r] = jnp.sum(COMP[r : r + 1])
+        comp_out[r] = jnp.sum(jnp.where(spot == r, COMP[0:1], 0.0))
 
     def out_copy(g, c):
         return pltpu.make_async_copy(
@@ -700,8 +701,8 @@
                 pltpu.VMEM((3, 24, DEEP), F32),
                 pltpu.VMEM((EZ, DEEP), BF16),
                 pltpu.VMEM((DEEP, EZ), BF16),
-                pltpu.VMEM((wide // 2, 8, 128), F32),
-                pltpu.VMEM((2 * narrow, 8, 128), F32),
+                pltpu.VMEM((wide // 2, 128), F32),
+                pltpu.VMEM((2 * narrow, 128), F32),
                 pltpu.SMEM((18,), F32),
                 sems((7,)),
                 sems((8,)), sems((8,)), sems((3,)), sems((3,)), sems((8,)), sems((8,)),

time: 40.9 us -> 38.9 us (0.951)
  Pallas kernels: 40.2 us -> 38.2 us
    pallas_call x1, Pallas kernels: 37.7 us -> 35.6 us  [local(): pl.pallas_call(functools.partial(kernel, wide, narrow), out_shape=passed,...]
where the time goes in v4:
time: 38.9 us; the launch traced here: 38.8 us
  Pallas kernels  38.2 us (98%)
  between operations  0.64 us (2%)
    pallas_call x1, Pallas kernels, local(): pl.pallas_call(functools.partial(kernel, wide, narrow), out_shape=passed,...  35.6 us
    pallas_call x1, Pallas kernels, local(): pl.pallas_call(finish, out_shape=(jax.ShapeDtypeStruct((9, EX, EY, EZ), F...  2.54 us

profile of v4, /device:TPU:1, one launch (start us, length us, event | category | flops | bytes accessed | tf_op | source)
XLA Modules:
  0.0 38.8 jit_solution(6921189415181901082)
XLA Ops:
  0.6 35.6 %shard_map.76 = (f32[12,3,3,32,128]{4,3,2,1,0:T(8,128)S(1)}, f32[9,4,16,128]{3,2,1,0:T(8,128)S(1)}, f32[8,128]{1,0:T(8,128)S(1)}, bf16[256,256]{1,0:T(8,128)(2,1)S(1)}) custom-call(f32[12,48,384]{2,1,0:T(8,128)} %design.1, s32[12,48,384]{2,1,0:T(8,128)} %passive.1, f32[9,4,16,128]{3,2,1,0:T(8,128)} %bitcast.2, s32[4,16,128]{2,1,0:T(8,128)} %support.1, ...), custom_call_target="tpu_custom_call" | custom-call | tf_op jit(solution)/shard_map/pallas_call | solution.py:674
  36.3 2.5 %shard_map.77 = (f32[9,4,16,128]{3,2,1,0:T(8,128)}, f32[3]{0:T(128)}, f32[12,48,384]{2,1,0:T(8,128)}) custom-call(f32[12,3,3,32,128]{4,3,2,1,0:T(8,128)S(1)} %get-tuple-element.10.GX, f32[9,4,16,128]{3,2,1,0:T(8,128)S(1)} %get-tuple-element.11.RES, f32[8,128]{1,0:T(8,128)S(1)} %get-tuple-element.12.COMP, bf16[256,256]{1,0:T(8,128)(2,1)S(1)} %get-tuple-element.13.BAND), custom_call_target="tpu_custom_call" | custom-call | tf_op jit(solution)/shard_map/pallas_call | solution.py:719

commit v5 on v4

--- a/solution.py
+++ b/solution.py
@@ -137,8 +137,8 @@
 def kernel(
     wide, narrow,
     design, passive, disp, support, loading,
-    GX, RES, COMP, BAND,
-    AH, AL, D, XF, PA, SW, BL, T, EN, ESP, V, M, FS, FXR, FYR, FDR, U, SU, LO, MOD, S3,
+    Y, RES, COMP, BAND,
+    AH, AL, D, XF, PA, SW, BL, T, EN, ESP, GX, V, M, FS, FXR, FYR, FDR, U, SU, LO, MOD, S3,
     WT, SPREAD, GATHER, AR1, AR2, RX,
     lsem, dss, drs, mss, mrs, bss, brs, ess, ers, fss, frs, sss, srs, a1s, a1r, a2s, a2r,
 ):
@@ -429,14 +429,12 @@
     z_step((1, 2))
     for message in fields[2:]:
         message.start()
-    fields[1].start()
     for message in (moves[0], holds[0], moves[2], holds[2]):
         message.wait_recv()
     moved(4)
     lax.fori_loop(0, 3, last_energies, 0)
-    for message in late:
+    for message in late + fields[:2]:
         message.start()
-    fields[0].start()
 
     def own_step(xe, _):
         sums = [None] * 3
@@ -559,10 +557,6 @@
         ESP[r, 5, 0:16] = block[80 * r + 16 : 80 * r + 32]
         for l in range(6):
             ESP[r, l, 16:24] = block[80 * r + 32 + 8 * l : 80 * r + 40 + 8 * l]
-    for message in fields[:2]:
-        message.wait_recv()
-    for l in (0, 15):
-        lax.fori_loop(l, l + 3, row_terms, 0)
     for message in fields[2:4]:
         message.wait_recv()
     lax.fori_loop(3, 15, column_terms, 0)
@@ -570,6 +564,40 @@
         message.wait_recv()
     for l in (0, 15):
         lax.fori_loop(l, l + 3, column_terms, 0)
+    for message in fields[:2]:
+        message.wait_recv()
+    for l in (0, 15):
+        lax.fori_loop(l, l + 3, row_terms, 0)
+
+    def back_step(r, _):
+        def x_back(m, _):
+            for t in range(3):
+                for c in range(3):
+                    lanes = slice(128 * c, 128 * c + 128)
+                    rows = slice(8 * t, 8 * t + 8)
+                    out = tent([T[r, x, m, rows, lanes] for x in range(18)])
+                    for x in range(ROWS):
+                        GX[x, m, c, 8 + 8 * t : 16 + 8 * t, :] = out[x]
+                        if t == 2:
+                            GX[x, m, c, 0:8, :] = out[x]
+            return 0
+
+        def y_back(x, _):
+            for t in range(2):
+                for c in range(3):
+                    out = tent(
+                        [GX[x, k % 3, c, pl.ds(8 + 8 * t + k // 3, 8), :] for k in range(-3, 6)]
+                    )
+                    for m in range(3):
+                        at = 16 * m + 8 * t
+                        Y[r, x, at : at + 8, 128 * c : 128 * c + 128] = out[m]
+            return 0
+
+        lax.fori_loop(0, 3, x_back, 0)
+        lax.fori_loop(0, ROWS, y_back, 0)
+        return 0
+
+    lax.fori_loop(0, 3, back_step, 0)
 
     for message in forces:
         message.wait_recv()
@@ -587,30 +615,7 @@
         RES[k] = ((load - stiff) if k % 3 == 2 else (0.0 - stiff)) * free
 
     whole2.wait_recv()
-    whole = jnp.sum(AR2[...], axis=0, keepdims=True)
-    COMP[...] = jnp.broadcast_to(whole, (8, 128))
-    scales = [
-        jnp.broadcast_to(-slope_scale(thresholds[r]) / whole[:, r : r + 1], (8, 128)) for r in range(3)
-    ]
-
-    def x_back(m, _):
-        for t in range(3):
-            for c in range(3):
-                lanes = slice(128 * c, 128 * c + 128)
-                rows = slice(8 * t, 8 * t + 8)
-                values = []
-                for x in range(18):
-                    v = T[0, x, m, rows, lanes] * scales[0]
-                    v = v + T[1, x, m, rows, lanes] * scales[1]
-                    values.append(v + T[2, x, m, rows, lanes] * scales[2])
-                out = tent(values)
-                for x in range(ROWS):
-                    GX[x, m, c, 8 + 8 * t : 16 + 8 * t, :] = out[x]
-                    if t == 2:
-                        GX[x, m, c, 0:8, :] = out[x]
-        return 0
-
-    lax.fori_loop(0, 3, x_back, 0)
+    COMP[...] = jnp.broadcast_to(jnp.sum(AR2[...], axis=0, keepdims=True), (8, 128))
 
     for message in moves + holds + designs + fields + energies + forces:
         message.wait_send()
@@ -618,7 +623,7 @@
     whole2.wait_send()
 
 
-def finish(GX, RES, COMP, BAND, res_out, comp_out, sens_out, AH, AL, OUT, osem):
+def finish(Y, RES, COMP, BAND, res_out, comp_out, sens_out, AH, AL, OUT, osem):
     res_copy = pltpu.make_async_copy(RES, res_out, osem.at[6])
     res_copy.start()
     spot = lax.broadcasted_iota(jnp.int32, (1, 128), 1)
@@ -632,18 +637,25 @@
             osem.at[3 * g + c],
         )
 
-    def y_back(x, _):
+    scales = [
+        jnp.broadcast_to(-slope_scale(thresholds[r]) / COMP[0:1, r : r + 1], (8, 128)) for r in range(3)
+    ]
+
+    def combine(x, _):
         parts = {}
-        for t in range(2):
-            for c in range(3):
-                out = tent([GX[x, k % 3, c, pl.ds(8 + 8 * t + k // 3, 8), :] for k in range(-3, 6)])
-                for m in range(3):
-                    parts[m, t, c] = out[m]
+        for m in range(3):
+            for t in range(2):
+                at = 16 * m + 8 * t
+                for c in range(3):
+                    lanes = slice(128 * c, 128 * c + 128)
+                    value = Y[0, x, at : at + 8, lanes] * scales[0]
+                    value = value + Y[1, x, at : at + 8, lanes] * scales[1]
+                    parts[m, t, c] = value + Y[2, x, at : at + 8, lanes] * scales[2]
         keep(AH, AL, x, parts)
         return 0
 
     for g in range(2):
-        lax.fori_loop(6 * g, 6 * g + 6, y_back, 0)
+        lax.fori_loop(6 * g, 6 * g + 6, combine, 0)
         z = banded(AH, AL, BAND, (2 * g, 2 * g + 1))
         for c in range(3):
             for xr in range(6):
@@ -666,7 +678,7 @@
         vmem = pl.BlockSpec(memory_space=pltpu.VMEM)
         hbm = pl.BlockSpec(memory_space=pltpu.MemorySpace.HBM)
         passed = (
-            jax.ShapeDtypeStruct((ROWS, 3, 3, 32, 128), F32),
+            jax.ShapeDtypeStruct((3, ROWS, COLS, DEEP), F32),
             jax.ShapeDtypeStruct((9, EX, EY, EZ), F32),
             jax.ShapeDtypeStruct((8, 128), F32),
             jax.ShapeDtypeStruct((256, 256), BF16),
@@ -687,6 +699,7 @@
                 pltpu.VMEM((3, 18, 3, 24, DEEP), F32),
                 pltpu.VMEM((3, 6, 32, 128), F32),
                 pltpu.VMEM((3, 6, 24, DEEP), F32),
+                pltpu.VMEM((ROWS, 3, 3, 32, 128), F32),
                 pltpu.VMEM((12, 24, 16, 128), F32),
                 pltpu.VMEM((9, 5, 24, 128), F32),
                 pltpu.VMEM((9, 5, 24, 128), F32),

time: 38.9 us -> 38.1 us (0.979)
  Pallas kernels: 38.2 us -> 37.4 us
    pallas_call x1, Pallas kernels: 35.6 us -> 34.9 us  [local(): pl.pallas_call(functools.partial(kernel, wide, narrow), out_shape=passed,...]
where the time goes in v5:
time: 38.1 us; the launch traced here: 38 us
  Pallas kernels  37.4 us (98%)
  between operations  0.64 us (2%)
    pallas_call x1, Pallas kernels, local(): pl.pallas_call(functools.partial(kernel, wide, narrow), out_shape=passed,...  34.9 us
    pallas_call x1, Pallas kernels, local(): pl.pallas_call(finish, out_shape=(jax.ShapeDtypeStruct((9, EX, EY, EZ), F...  2.44 us

profile of v5, /device:TPU:1, one launch (start us, length us, event | category | flops | bytes accessed | tf_op | source)
XLA Modules:
  0.0 38.0 jit_solution(1619452317376830679)
XLA Ops:
  0.6 34.9 %shard_map.76 = (f32[3,12,48,384]{3,2,1,0:T(8,128)S(1)}, f32[9,4,16,128]{3,2,1,0:T(8,128)S(1)}, f32[8,128]{1,0:T(8,128)S(1)}, bf16[256,256]{1,0:T(8,128)(2,1)S(1)}) custom-call(f32[12,48,384]{2,1,0:T(8,128)} %design.1, s32[12,48,384]{2,1,0:T(8,128)} %passive.1, f32[9,4,16,128]{3,2,1,0:T(8,128)} %bitcast.2, s32[4,16,128]{2,1,0:T(8,128)} %support.1, ...), custom_call_target="tpu_custom_call" | custom-call | tf_op jit(solution)/shard_map/pallas_call | solution.py:686
  35.6 2.4 %shard_map.77 = (f32[9,4,16,128]{3,2,1,0:T(8,128)}, f32[3]{0:T(128)}, f32[12,48,384]{2,1,0:T(8,128)}) custom-call(f32[3,12,48,384]{3,2,1,0:T(8,128)S(1)} %get-tuple-element.10.Y, f32[9,4,16,128]{3,2,1,0:T(8,128)S(1)} %get-tuple-element.11.RES, f32[8,128]{1,0:T(8,128)S(1)} %get-tuple-element.12.COMP, bf16[256,256]{1,0:T(8,128)(2,1)S(1)} %get-tuple-element.13.BAND), custom_call_target="tpu_custom_call" | custom-call | tf_op jit(solution)/shard_map/pallas_call | solution.py:732

commit v6 on v5

--- a/solution.py
+++ b/solution.py
@@ -253,7 +253,7 @@
     forces.append(Message(FS.at[:, 4, 16:17, :], FDR.at[:, 0:1, :], fss.at[2], frs.at[2], 1, 1))
 
     pl.semaphore_wait(barrier, total)
-    for message in moves[1:] + holds[1:] + designs[2:] + designs[:2] + moves[:1] + holds[:1]:
+    for message in moves + holds + designs[2:] + designs[:2]:
         message.start()
 
     def near(shape):
@@ -383,9 +383,11 @@
         return 0
 
     lax.fori_loop(0, 9, inner_energies, 0)
-    early = [message for message, d in zip(energies, DIRS) if d[0] < 0]
-    late = [message for message, d in zip(energies, DIRS) if d[0] >= 0]
-    for message in early:
+    for message in (moves[0], holds[0], moves[2], holds[2]):
+        message.wait_recv()
+    moved(4)
+    lax.fori_loop(0, 3, last_energies, 0)
+    for message in energies:
         message.start()
 
     loads[2].wait()
@@ -427,13 +429,7 @@
 
     z_step((0, 3))
     z_step((1, 2))
-    for message in fields[2:]:
-        message.start()
-    for message in (moves[0], holds[0], moves[2], holds[2]):
-        message.wait_recv()
-    moved(4)
-    lax.fori_loop(0, 3, last_energies, 0)
-    for message in late + fields[:2]:
+    for message in fields[2:] + fields[:2]:
         message.start()
 
     def own_step(xe, _):

time: 38.1 us -> 37.9 us (level)
  no operation moved by 1% of the time
where the time goes in v6:
time: 37.9 us; the launch traced here: 37.8 us
  Pallas kernels  37.1 us (98%)
  between operations  0.64 us (2%)
    pallas_call x1, Pallas kernels, local(): pl.pallas_call(functools.partial(kernel, wide, narrow), out_shape=passed,...  34.7 us
    pallas_call x1, Pallas kernels, local(): pl.pallas_call(finish, out_shape=(jax.ShapeDtypeStruct((9, EX, EY, EZ), F...  2.44 us

profile of v6, /device:TPU:1, one launch (start us, length us, event | category | flops | bytes accessed | tf_op | source)
XLA Modules:
  0.0 37.8 jit_solution(14716959312545429595)
XLA Ops:
  0.6 34.7 %shard_map.76 = (f32[3,12,48,384]{3,2,1,0:T(8,128)S(1)}, f32[9,4,16,128]{3,2,1,0:T(8,128)S(1)}, f32[8,128]{1,0:T(8,128)S(1)}, bf16[256,256]{1,0:T(8,128)(2,1)S(1)}) custom-call(f32[12,48,384]{2,1,0:T(8,128)} %design.1, s32[12,48,384]{2,1,0:T(8,128)} %passive.1, f32[9,4,16,128]{3,2,1,0:T(8,128)} %bitcast.2, s32[4,16,128]{2,1,0:T(8,128)} %support.1, ...), custom_call_target="tpu_custom_call" | custom-call | tf_op jit(solution)/shard_map/pallas_call | solution.py:682
  35.3 2.4 %shard_map.77 = (f32[9,4,16,128]{3,2,1,0:T(8,128)}, f32[3]{0:T(128)}, f32[12,48,384]{2,1,0:T(8,128)}) custom-call(f32[3,12,48,384]{3,2,1,0:T(8,128)S(1)} %get-tuple-element.10.Y, f32[9,4,16,128]{3,2,1,0:T(8,128)S(1)} %get-tuple-element.11.RES, f32[8,128]{1,0:T(8,128)S(1)} %get-tuple-element.12.COMP, bf16[256,256]{1,0:T(8,128)(2,1)S(1)} %get-tuple-element.13.BAND), custom_call_target="tpu_custom_call" | custom-call | tf_op jit(solution)/shard_map/pallas_call | solution.py:728

commit v7 on v6

--- a/solution.py
+++ b/solution.py
@@ -427,8 +427,7 @@
                         lanes = slice(128 * c, 128 * c + 128)
                         BL[x + 3, m, 8:24, lanes] = z[c][at : at + 16] * SW[x, m, :, lanes]
 
-    z_step((0, 3))
-    z_step((1, 2))
+    z_step((0, 1, 2, 3))
     for message in fields[2:] + fields[:2]:
         message.start()
 
@@ -622,9 +621,6 @@
 def finish(Y, RES, COMP, BAND, res_out, comp_out, sens_out, AH, AL, OUT, osem):
     res_copy = pltpu.make_async_copy(RES, res_out, osem.at[6])
     res_copy.start()
-    spot = lax.broadcasted_iota(jnp.int32, (1, 128), 1)
-    for r in range(3):
-        comp_out[r] = jnp.sum(jnp.where(spot == r, COMP[0:1], 0.0))
 
     def out_copy(g, c):
         return pltpu.make_async_copy(
@@ -660,6 +656,9 @@
                         at = 16 * (3 * xr + m) + 8 * t
                         OUT[6 * g + xr, c, pl.ds(24 * t + m, 8, stride=3), :] = z[c][at : at + 8]
             out_copy(g, c).start()
+    spot = lax.broadcasted_iota(jnp.int32, (1, 128), 1)
+    for r in range(3):
+        comp_out[r] = jnp.sum(jnp.where(spot == r, COMP[0:1], 0.0))
     res_copy.wait()
     for g in range(2):
         for c in range(3):

time: 37.9 us -> 37.8 us (level)
  no operation moved by 1% of the time
where the time goes in v7:
time: 37.8 us; the launch traced here: 37.7 us
  Pallas kernels  37.1 us (98%)
  between operations  0.64 us (2%)
    pallas_call x1, Pallas kernels, local(): pl.pallas_call(functools.partial(kernel, wide, narrow), out_shape=passed,...  34.7 us
    pallas_call x1, Pallas kernels, local(): pl.pallas_call(finish, out_shape=(jax.ShapeDtypeStruct((9, EX, EY, EZ), F...  2.43 us

profile of v7, /device:TPU:1, one launch (start us, length us, event | category | flops | bytes accessed | tf_op | source)
XLA Modules:
  0.0 37.7 jit_solution(4922105469889398064)
XLA Ops:
  0.6 34.7 %shard_map.76 = (f32[3,12,48,384]{3,2,1,0:T(8,128)S(1)}, f32[9,4,16,128]{3,2,1,0:T(8,128)S(1)}, f32[8,128]{1,0:T(8,128)S(1)}, bf16[256,256]{1,0:T(8,128)(2,1)S(1)}) custom-call(f32[12,48,384]{2,1,0:T(8,128)} %design.1, s32[12,48,384]{2,1,0:T(8,128)} %passive.1, f32[9,4,16,128]{3,2,1,0:T(8,128)} %bitcast.2, s32[4,16,128]{2,1,0:T(8,128)} %support.1, ...), custom_call_target="tpu_custom_call" | custom-call | tf_op jit(solution)/shard_map/pallas_call | solution.py:681
  35.3 2.4 %shard_map.77 = (f32[9,4,16,128]{3,2,1,0:T(8,128)}, f32[3]{0:T(128)}, f32[12,48,384]{2,1,0:T(8,128)}) custom-call(f32[3,12,48,384]{3,2,1,0:T(8,128)S(1)} %get-tuple-element.10.Y, f32[9,4,16,128]{3,2,1,0:T(8,128)S(1)} %get-tuple-element.11.RES, f32[8,128]{1,0:T(8,128)S(1)} %get-tuple-element.12.COMP, bf16[256,256]{1,0:T(8,128)(2,1)S(1)} %get-tuple-element.13.BAND), custom_call_target="tpu_custom_call" | custom-call | tf_op jit(solution)/shard_map/pallas_call | solution.py:727

commit v8 on v7

--- a/solution.py
+++ b/solution.py
@@ -253,7 +253,7 @@
     forces.append(Message(FS.at[:, 4, 16:17, :], FDR.at[:, 0:1, :], fss.at[2], frs.at[2], 1, 1))
 
     pl.semaphore_wait(barrier, total)
-    for message in moves + holds + designs[2:] + designs[:2]:
+    for message in moves[1:] + holds[1:] + designs[2:] + moves[:1] + holds[:1] + designs[:2]:
         message.start()
 
     def near(shape):

time: 37.8 us -> 38.3 us (1.013)
  Pallas kernels: 37.1 us -> 37.6 us
    pallas_call x1, Pallas kernels: 34.7 us -> 35.1 us  [local(): pl.pallas_call(functools.partial(kernel, wide, narrow), out_shape=passed,...]
where the time goes in v8:
time: 38.3 us; the launch traced here: 38.2 us
  Pallas kernels  37.6 us (98%)
  between operations  0.64 us (2%)
    pallas_call x1, Pallas kernels, local(): pl.pallas_call(functools.partial(kernel, wide, narrow), out_shape=passed,...  35.1 us
    pallas_call x1, Pallas kernels, local(): pl.pallas_call(finish, out_shape=(jax.ShapeDtypeStruct((9, EX, EY, EZ), F...  2.43 us

profile of v8, /device:TPU:1, one launch (start us, length us, event | category | flops | bytes accessed | tf_op | source)
XLA Modules:
  0.0 38.2 jit_solution(16291444714342914758)
XLA Ops:
  0.6 35.1 %shard_map.76 = (f32[3,12,48,384]{3,2,1,0:T(8,128)S(1)}, f32[9,4,16,128]{3,2,1,0:T(8,128)S(1)}, f32[8,128]{1,0:T(8,128)S(1)}, bf16[256,256]{1,0:T(8,128)(2,1)S(1)}) custom-call(f32[12,48,384]{2,1,0:T(8,128)} %design.1, s32[12,48,384]{2,1,0:T(8,128)} %passive.1, f32[9,4,16,128]{3,2,1,0:T(8,128)} %bitcast.2, s32[4,16,128]{2,1,0:T(8,128)} %support.1, ...), custom_call_target="tpu_custom_call" | custom-call | tf_op jit(solution)/shard_map/pallas_call | solution.py:681
  35.8 2.4 %shard_map.77 = (f32[9,4,16,128]{3,2,1,0:T(8,128)}, f32[3]{0:T(128)}, f32[12,48,384]{2,1,0:T(8,128)}) custom-call(f32[3,12,48,384]{3,2,1,0:T(8,128)S(1)} %get-tuple-element.10.Y, f32[9,4,16,128]{3,2,1,0:T(8,128)S(1)} %get-tuple-element.11.RES, f32[8,128]{1,0:T(8,128)S(1)} %get-tuple-element.12.COMP, bf16[256,256]{1,0:T(8,128)(2,1)S(1)} %get-tuple-element.13.BAND), custom_call_target="tpu_custom_call" | custom-call | tf_op jit(solution)/shard_map/pallas_call | solution.py:727
